TPU v7x, 32 devices: a whole 2x2x4 slice. The times are simulated.
32 devices in a mesh: pipe: 2 (over y), expert: 16 (over z, x, core).
Axes of the slice: x: 2, y: 2, z: 4, core: 2. Of those that a mesh axis runs over, the one named last changes fastest.
Arguments:
- resident_batchlets: bfloat16 [2, 256, 2048], P('pipe', 'expert'), may hold values from -6 to 6
- incoming_batchlets: bfloat16 [1, 256, 2048], P(None, 'expert'), may hold values from -6 to 6
- segment_rms_gain: float32 [2, 2048], P('pipe'), may hold values from 0.25 to 1.75
- gating_projection: bfloat16 [16, 2048, 768], P('expert'), may hold values from -0.125 to 0.125
- expanding_projection: bfloat16 [16, 2048, 768], P('expert'), may hold values from -0.125 to 0.125
- contracting_projection: bfloat16 [16, 768, 2048], P('expert'), may hold values from -0.21875 to 0.21875
- picked_specialist_ids: int32 [2, 2, 256, 8], P(None, 'pipe', 'expert'), may hold values from 0 to 15, all different within a row; in each aligned block of 16 rows (0 to 15, 16 to 31, ..., all dimensions but the last counted through in order) at most 9 rows name the same one
- blend_factors: float32 [2, 2, 256, 8], P(None, 'pipe', 'expert'), may hold values from 0.02 to 0.25
Outputs:
- stash: bfloat16 [2, 2, 256, 2048], P(None, 'pipe', 'expert')
Inputs may be any that keep to these rules, and one draw needn't show every extreme that they name: `picked_specialist_ids`: each row names 8 different experts. Among the rows of one device (aligned blocks of 16 rows), no expert is named more than 9 times, and in some blocks one expert is named exactly 9 times.
All inputs are finite; a program needn't handle non-finite values.
Results may differ from a plain program's by a relative error of at most 0.005.
Values may be sent and summed in bfloat16 or wider, within the bound.
No kernel may reach another device: no remote copies, remote signals or barrier semaphores. Data moves between devices by JAX's collectives and lax.ppermute only.
A program may use at most 64 MiB of HBM per device.

v0:
```python
import jax
import jax.numpy as jnp
from jax import lax
from jax.sharding import PartitionSpec as P

epsilon = 1e-06


def shifted(value, axis, steps):
    count = lax.axis_size(axis)
    first, last = (max(0, -steps), min(count, count - steps))
    return lax.ppermute(value, axis, [(source, source + steps) for source in range(first, last)])


def normalize(hidden_rows, gain_row):
    values = hidden_rows.astype(jnp.float32)
    scale = lax.rsqrt(jnp.mean(values * values, axis=-1, keepdims=True) + epsilon)
    return (values * scale * gain_row).astype(jnp.bfloat16)


def swiglu(tile_rows, gate_matrix, up_matrix, down_matrix):
    gate_part = jnp.dot(tile_rows, gate_matrix, preferred_element_type=jnp.float32)
    up_part = jnp.dot(tile_rows, up_matrix, preferred_element_type=jnp.float32)
    inner = (jax.nn.silu(gate_part) * up_part).astype(jnp.bfloat16)
    return jnp.dot(inner, down_matrix, preferred_element_type=jnp.float32).astype(jnp.bfloat16)


def expert_rows(received, alive_flags, gate_matrix, up_matrix, down_matrix):
    sources = received.shape[0]
    item_count = received.shape[1]
    feature_count = received.shape[2]
    row_total = sources * item_count
    flat_rows = received.reshape(row_total, feature_count)
    flat_alive = alive_flags.reshape(row_total)
    result = swiglu(flat_rows, gate_matrix, up_matrix, down_matrix) * flat_alive[:, None].astype(
        jnp.bfloat16
    )
    return result.reshape(sources, item_count, feature_count)


def local(
    resident_batchlets,
    incoming_batchlets,
    segment_rms_gain,
    gating_projection,
    expanding_projection,
    contracting_projection,
    picked_specialist_ids,
    blend_factors,
):
    section = lax.axis_index("pipe")
    experts = lax.axis_size("expert") * gating_projection.shape[0]
    segment_items = resident_batchlets.shape[1]
    top_count = picked_specialist_ids.shape[3]
    capacity = min(segment_items, -(-(segment_items * top_count) // experts) + 1)
    gain_row = segment_rms_gain[0]
    gate_matrix = gating_projection[0]
    up_matrix = expanding_projection[0]
    down_matrix = contracting_projection[0]
    expert_range = jnp.arange(experts, dtype=jnp.int32)
    slot_range = jnp.arange(experts * capacity, dtype=jnp.int32)
    capacity_range = jnp.arange(capacity, dtype=jnp.int32)
    carry_value = resident_batchlets[0]
    outputs = []
    for moment in range(picked_specialist_ids.shape[0]):
        normed = normalize(carry_value, gain_row)
        flat_ids = picked_specialist_ids[moment, 0].reshape(-1)
        onehot = (flat_ids[:, None] == expert_range[None, :]).astype(jnp.int32)
        earlier = jnp.cumsum(onehot, axis=0) - onehot
        position = jnp.sum(earlier * onehot, axis=1)
        target = flat_ids * capacity + position
        counts = jnp.sum(onehot, axis=0)
        alive_flags = (capacity_range[None, :] < counts[:, None]).astype(jnp.int32)
        matches = target.reshape(segment_items, top_count)[None, :, :] == slot_range[:, None, None]
        selector = jnp.any(matches, axis=2).astype(jnp.bfloat16)
        outgoing = jnp.dot(selector, normed, preferred_element_type=jnp.float32).astype(
            jnp.bfloat16
        )
        outgoing = outgoing.reshape(experts, capacity, normed.shape[1])
        arrived = lax.all_to_all(outgoing, "expert", split_axis=0, concat_axis=0, tiled=True)
        arrived_flags = lax.all_to_all(
            alive_flags, "expert", split_axis=0, concat_axis=0, tiled=True
        )
        answered = expert_rows(arrived, arrived_flags, gate_matrix, up_matrix, down_matrix)
        returned = lax.all_to_all(answered, "expert", split_axis=0, concat_axis=0, tiled=True)
        flat_back = returned.reshape(experts * capacity, normed.shape[1])
        values = jnp.take(flat_back, target, axis=0).reshape(
            segment_items, top_count, normed.shape[1]
        )
        mixed_sum = jnp.sum(
            values.astype(jnp.float32) * blend_factors[moment, 0][:, :, None], axis=1
        )
        stepped = (carry_value.astype(jnp.float32) + mixed_sum).astype(jnp.bfloat16)
        outputs.append(stepped)
        if moment + 1 < picked_specialist_ids.shape[0]:
            arrived_state = shifted(stepped, "pipe", 1)
            carry_value = jnp.where(section == 0, incoming_batchlets[moment], arrived_state)
    return jnp.stack(outputs, axis=0)[:, None]


def solution(mesh):
    in_specs = (
        P("pipe", "expert", None),
        P(None, "expert", None),
        P("pipe", None),
        P("expert", None, None),
        P("expert", None, None),
        P("expert", None, None),
        P(None, "pipe", "expert", None),
        P(None, "pipe", "expert", None),
    )
    out_specs = P(None, "pipe", "expert", None)
    return jax.shard_map(local, mesh=mesh, in_specs=in_specs, out_specs=out_specs, check_vma=False)
```

profile of v0, /device:TPU:0, one launch (start us, length us, event | category | flops | bytes accessed | tf_op | source)
XLA Modules:
  0.0 191.4 jit_solution(15325854582501950139)
XLA Ops:
  0.0 0.9 fusion.81
  0.9 0.1 copy.33
  0.9 0.1 eq.59
  1.0 0.1 fusion.76
  1.1 0.2 reduce_window_sum.17
  1.3 0.2 fusion.77
  1.5 0.7 compare_convert_fusion.1
  2.2 7.4 %all-to-all-start.1 = ((s32[16,1,9]{2,1,0:T(1,128)}), s32[16,1,9]{2,1,0:T(1,128)S(1)}, u32[]{:S(2)}, u32[]{:S(2)}) async-start(s32[16,1,9]{2,1,0:T(1,128)} %compare_convert_fusion.1), calls=%async_computation.1 | async-start | bytes 16384 | tf_op jit(solution)/shard_map/all_to_all | solution.py:81
  9.6 1.0 fusion.57
  10.5 0.1 copy.37
  10.6 0.1 eq.67
  10.7 0.1 fusion.72
  10.8 0.2 reduce_window_sum.18
  11.0 0.2 fusion.78
  11.1 0.1 reduce_sum.85
  11.2 0.1 copy.38
  11.3 0.1 reduce_sum.79
  11.4 0.1 copy.34
  11.5 0.7 bitcast_add_fusion.1
  12.2 0.1 copy.35
  12.3 0.1 fusion.66
  12.4 2.0 %convolution_convert_fusion.1 = bf16[144,2048]{1,0:T(8,128)(2,1)} fusion(pred[144,16]{0,1:T(8,128)(4,1)S(1)} %fusion.66, bf16[1,16,2048]{2,1,0:T(8,128)(2,1)} %param.10, f32[2048]{0:T(1024)} %bitcast.86, f32[16]{0:T(128)S(1)} %add_rsqrt_fusion.1), kind=kOutput, calls=%fused_computation.17 | convolution fusion | flops 9863168 | bytes 665920 | tf_op jit(solution)/shard_map/dot_general | solution.py:76
  14.4 2.3 %reshape.164 = bf16[16,9,2048]{2,1,0:T(8,128)(2,1)} reshape(bf16[144,2048]{1,0:T(8,128)(2,1)} %convolution_convert_fusion.1) | data formatting | bytes 1179648 | tf_op jit(solution)/shard_map/reshape | solution.py:79
  16.7 0.0 all-to-all-done.1
  16.7 6.1 %all-to-all-start = ((bf16[16,9,2048]{2,1,0:T(8,128)(2,1)}), bf16[16,9,2048]{2,1,0:T(8,128)(2,1)}, u32[]{:S(2)}, u32[]{:S(2)}) async-start(bf16[16,9,2048]{2,1,0:T(8,128)(2,1)} %reshape.164), calls=%async_computation | async-start | bytes 2097152 | tf_op jit(solution)/shard_map/all_to_all | solution.py:80
  22.8 0.1 convert_element_type.119
  22.9 22.8 %all-to-all-done = bf16[16,9,2048]{2,1,0:T(8,128)(2,1)} async-done(((bf16[16,9,2048]{2,1,0:T(8,128)(2,1)}), bf16[16,9,2048]{2,1,0:T(8,128)(2,1)}, u32[]{:S(2)}, u32[]{:S(2)}) %all-to-all-start) | async-done | bytes 589856 | tf_op jit(solution)/shard_map/all_to_all | solution.py:80
  45.8 2.3 %reshape.165 = bf16[144,2048]{1,0:T(8,128)(2,1)} reshape(bf16[16,9,2048]{2,1,0:T(8,128)(2,1)} %all-to-all-done) | data formatting | bytes 1179648 | tf_op jit(solution)/shard_map/reshape | solution.py:33
  48.1 3.5 %fusion.10 = f32[144,768]{1,0:T(8,128)} fusion(bf16[144,2048]{1,0:T(8,128)(2,1)} %reshape.165, bf16[1,2048,768]{2,1,0:T(8,128)(2,1)} %param.13), kind=kOutput, calls=%fused_computation.12 | convolution fusion | flops 452984832 | bytes 4177920 | tf_op jit(solution)/shard_map/dot_general | solution.py:22
  51.5 4.3 %fusion.21 = bf16[144,2048]{1,0:T(8,128)(2,1)} fusion(bf16[1,768,2048]{2,1,0:T(8,128)(2,1)S(1)} %copy-done, bf16[144,2048]{1,0:T(8,128)(2,1)} %reshape.165, bf16[1,2048,768]{2,1,0:T(8,128)(2,1)} %param.14, f32[144,768]{1,0:T(8,128)} %fusion.10, bf16[144]{0:T(256)(128)(2,1)S(1)} %convert_element_type.119), kind=kOutput, calls=%fused_computation.19 | convolution fusion | flops 908107776 | bytes 7913760 | tf_op jit(solution)/shard_map/dot_general | solution.py:25
  55.8 2.3 %reshape.166 = bf16[16,9,2048]{2,1,0:T(8,128)(2,1)} reshape(bf16[144,2048]{1,0:T(8,128)(2,1)} %fusion.21) | data formatting | bytes 1179648 | tf_op jit(solution)/shard_map/reshape | solution.py:38
  58.2 6.8 %all-to-all-start.2 = ((bf16[16,9,2048]{2,1,0:T(8,128)(2,1)}), bf16[16,9,2048]{2,1,0:T(8,128)(2,1)}, u32[]{:S(2)}, u32[]{:S(2)}) async-start(bf16[16,9,2048]{2,1,0:T(8,128)(2,1)} %reshape.166), calls=%async_computation.2 | async-start | bytes 2097152 | tf_op jit(solution)/shard_map/all_to_all | solution.py:85
  65.0 0.0 copy-done.4
  65.1 0.1 copy.36
  65.1 0.1 copy.39
  65.2 0.7 compare_convert_fusion
  65.9 22.1 %all-to-all-done.2 = bf16[16,9,2048]{2,1,0:T(8,128)(2,1)} async-done(((bf16[16,9,2048]{2,1,0:T(8,128)(2,1)}), bf16[16,9,2048]{2,1,0:T(8,128)(2,1)}, u32[]{:S(2)}, u32[]{:S(2)}) %all-to-all-start.2) | async-done | bytes 589856 | tf_op jit(solution)/shard_map/all_to_all | solution.py:85
  88.0 6.8 %all-to-all-start.4 = ((s32[16,1,9]{2,1,0:T(1,128)}), s32[16,1,9]{2,1,0:T(1,128)S(1)}, u32[]{:S(2)}, u32[]{:S(2)}) async-start(s32[16,1,9]{2,1,0:T(1,128)} %compare_convert_fusion), calls=%async_computation.4 | async-start | bytes 16384 | tf_op jit(solution)/shard_map/all_to_all | solution.py:81
  94.8 0.0 copy-start.1
  94.8 2.3 %reshape.167 = bf16[144,2048]{1,0:T(8,128)(2,1)} reshape(bf16[16,9,2048]{2,1,0:T(8,128)(2,1)} %all-to-all-done.2) | data formatting | bytes 1179648 | tf_op jit(solution)/shard_map/reshape | solution.py:86
  97.1 3.4 %gather_fusion = bf16[128,2048]{1,0:T(8,128)(2,1)} fusion(bf16[144,2048]{1,0:T(8,128)(2,1)} %reshape.167, s32[1024]{0:T(1024)S(1)} %pad_clamp_fusion.1), kind=kCustom, calls=%fused_computation.clone | custom fusion | bytes 1049088 | tf_op jit(solution)/shard_map/jit(_take)/gather | solution.py:87
  100.5 2.1 %fusion.37 = f32[16,2048]{1,0:T(8,128)S(1)} fusion(bf16[128,2048]{1,0:T(8,128)(2,1)} %gather_fusion, f32[16,8]{1,0:T(8,128)S(1)} %copy.36, pred[128]{0:T(512)(128)(4,1)S(1)} %get-tuple-element.14), kind=kLoop, calls=%fused_computation.27 | loop fusion | flops 1015808 | bytes 656000 | tf_op jit(solution)/shard_map/reduce_sum | solution.py:90
  102.7 0.0 copy-done.1
  102.7 3.4 %collective-permute-start = (bf16[16,2048]{1,0:T(8,128)(2,1)S(1)}, bf16[16,2048]{1,0:T(8,128)(2,1)S(1)}, u32[]{:S(2)}, u32[]{:S(2)}) collective-permute-start(bf16[16,2048]{1,0:T(8,128)(2,1)S(1)} %fusion.60), channel_id=1, source_target_pairs={{0,16},{1,17},{2,18},{3,19},{4,20},{5,21},{6,22},{7,23},{8,24},{9,... | collective-permute-start | bytes 196616 | tf_op jit(solution)/shard_map/ppermute | solution.py:12
  106.1 0.1 fusion.67
  106.3 1.8 collective-permute-done
  108.0 0.1 fusion.62
  108.2 1.2 convolution_convert_fusion
  109.4 2.3 %reshape.168 = bf16[16,9,2048]{2,1,0:T(8,128)(2,1)} reshape(bf16[144,2048]{1,0:T(8,128)(2,1)} %convolution_convert_fusion) | data formatting | bytes 1179648 | tf_op jit(solution)/shard_map/reshape | solution.py:79
  111.7 0.0 all-to-all-done.4
  111.7 6.0 %all-to-all-start.3 = ((bf16[16,9,2048]{2,1,0:T(8,128)(2,1)}), bf16[16,9,2048]{2,1,0:T(8,128)(2,1)}, u32[]{:S(2)}, u32[]{:S(2)}) async-start(bf16[16,9,2048]{2,1,0:T(8,128)(2,1)} %reshape.168), calls=%async_computation.3 | async-start | bytes 2097152 | tf_op jit(solution)/shard_map/all_to_all | solution.py:80
  117.8 0.1 convert_element_type.132
  117.9 22.8 %all-to-all-done.3 = bf16[16,9,2048]{2,1,0:T(8,128)(2,1)} async-done(((bf16[16,9,2048]{2,1,0:T(8,128)(2,1)}), bf16[16,9,2048]{2,1,0:T(8,128)(2,1)}, u32[]{:S(2)}, u32[]{:S(2)}) %all-to-all-start.3) | async-done | bytes 589856 | tf_op jit(solution)/shard_map/all_to_all | solution.py:80
  140.7 2.3 %reshape.169 = bf16[144,2048]{1,0:T(8,128)(2,1)} reshape(bf16[16,9,2048]{2,1,0:T(8,128)(2,1)} %all-to-all-done.3) | data formatting | bytes 1179648 | tf_op jit(solution)/shard_map/reshape | solution.py:33
  143.0 3.5 %fusion.8 = f32[144,768]{1,0:T(8,128)} fusion(bf16[144,2048]{1,0:T(8,128)(2,1)} %reshape.169, bf16[1,2048,768]{2,1,0:T(8,128)(2,1)} %param.13), kind=kOutput, calls=%fused_computation.10 | convolution fusion | flops 452984832 | bytes 4177920 | tf_op jit(solution)/shard_map/dot_general | solution.py:22
  146.5 4.3 %fusion.18 = bf16[144,2048]{1,0:T(8,128)(2,1)} fusion(bf16[1,768,2048]{2,1,0:T(8,128)(2,1)S(1)} %copy-done, bf16[144,2048]{1,0:T(8,128)(2,1)} %reshape.169, bf16[1,2048,768]{2,1,0:T(8,128)(2,1)} %param.14, f32[144,768]{1,0:T(8,128)} %fusion.8, bf16[144]{0:T(256)(128)(2,1)S(1)} %convert_element_type.132), kind=kOutput, calls=%fused_computation.18 | convolution fusion | flops 908107776 | bytes 7913760 | tf_op jit(solution)/shard_map/dot_general | solution.py:25
  150.8 2.3 %reshape.170 = bf16[16,9,2048]{2,1,0:T(8,128)(2,1)} reshape(bf16[144,2048]{1,0:T(8,128)(2,1)} %fusion.18) | data formatting | bytes 1179648 | tf_op jit(solution)/shard_map/reshape | solution.py:38
  153.1 6.8 %all-to-all-start.5 = ((bf16[16,9,2048]{2,1,0:T(8,128)(2,1)}), bf16[16,9,2048]{2,1,0:T(8,128)(2,1)}, u32[]{:S(2)}, u32[]{:S(2)}) async-start(bf16[16,9,2048]{2,1,0:T(8,128)(2,1)} %reshape.170), calls=%async_computation.5 | async-start | bytes 2097152 | tf_op jit(solution)/shard_map/all_to_all | solution.py:85
  160.0 0.1 copy.40
  160.1 22.8 %all-to-all-done.5 = bf16[16,9,2048]{2,1,0:T(8,128)(2,1)} async-done(((bf16[16,9,2048]{2,1,0:T(8,128)(2,1)}), bf16[16,9,2048]{2,1,0:T(8,128)(2,1)}, u32[]{:S(2)}, u32[]{:S(2)}) %all-to-all-start.5) | async-done | bytes 589856 | tf_op jit(solution)/shard_map/all_to_all | solution.py:85
  182.9 2.3 %reshape.171 = bf16[144,2048]{1,0:T(8,128)(2,1)} reshape(bf16[16,9,2048]{2,1,0:T(8,128)(2,1)} %all-to-all-done.5) | data formatting | bytes 1179648 | tf_op jit(solution)/shard_map/reshape | solution.py:86
  185.2 3.4 %gather_fusion.1 = bf16[128,2048]{1,0:T(8,128)(2,1)} fusion(bf16[144,2048]{1,0:T(8,128)(2,1)} %reshape.171, s32[1024]{0:T(1024)S(1)} %pad_clamp_fusion), kind=kCustom, calls=%fused_computation.1.clone | custom fusion | bytes 1049088 | tf_op jit(solution)/shard_map/jit(_take)/gather | solution.py:87
  188.6 2.1 %fusion.36 = f32[16,2048]{1,0:T(8,128)S(1)} fusion(bf16[128,2048]{1,0:T(8,128)(2,1)} %gather_fusion.1, f32[16,8]{1,0:T(8,128)S(1)} %copy.40, pred[128]{0:T(512)(128)(4,1)S(1)} %get-tuple-element.10), kind=kLoop, calls=%fused_computation.25 | loop fusion | flops 1015808 | bytes 656000 | tf_op jit(solution)/shard_map/reduce_sum | solution.py:90
  190.7 0.7 maximum_bitcast_fusion
  (19 shorter events, 0.2 us)
Async XLA Ops:
  0.0 51.5 %copy-start = (bf16[1,768,2048]{2,1,0:T(8,128)(2,1)S(1)}, bf16[1,768,2048]{2,1,0:T(8,128)(2,1)}, u32[]{:S(2)}) copy-start(bf16[1,768,2048]{2,1,0:T(8,128)(2,1)} %param.15) | copy-start | bytes 9437188
  2.2 14.6 %all-to-all-start.1 = ((s32[16,1,9]{2,1,0:T(1,128)}), s32[16,1,9]{2,1,0:T(1,128)S(1)}, u32[]{:S(2)}, u32[]{:S(2)}) async-start(s32[16,1,9]{2,1,0:T(1,128)} %compare_convert_fusion.1), calls=%async_computation.1 | async-start | bytes 16384 | tf_op jit(solution)/shard_map/all_to_all | solution.py:81
  16.7 29.0 %all-to-all-start = ((bf16[16,9,2048]{2,1,0:T(8,128)(2,1)}), bf16[16,9,2048]{2,1,0:T(8,128)(2,1)}, u32[]{:S(2)}, u32[]{:S(2)}) async-start(bf16[16,9,2048]{2,1,0:T(8,128)(2,1)} %reshape.164), calls=%async_computation | async-start | bytes 2097152 | tf_op jit(solution)/shard_map/all_to_all | solution.py:80
  55.8 9.2 %copy-start.4 = (f32[2,1,16,8]{2,3,1,0:T(8,128)S(1)}, f32[2,1,16,8]{2,3,1,0:T(8,128)}, u32[]{:S(2)}) copy-start(f32[2,1,16,8]{2,3,1,0:T(8,128)} %param.17) | copy-start | bytes 3076
  58.2 29.8 %all-to-all-start.2 = ((bf16[16,9,2048]{2,1,0:T(8,128)(2,1)}), bf16[16,9,2048]{2,1,0:T(8,128)(2,1)}, u32[]{:S(2)}, u32[]{:S(2)}) async-start(bf16[16,9,2048]{2,1,0:T(8,128)(2,1)} %reshape.166), calls=%async_computation.2 | async-start | bytes 2097152 | tf_op jit(solution)/shard_map/all_to_all | solution.py:85
  88.0 23.7 %all-to-all-start.4 = ((s32[16,1,9]{2,1,0:T(1,128)}), s32[16,1,9]{2,1,0:T(1,128)S(1)}, u32[]{:S(2)}, u32[]{:S(2)}) async-start(s32[16,1,9]{2,1,0:T(1,128)} %compare_convert_fusion), calls=%async_computation.4 | async-start | bytes 16384 | tf_op jit(solution)/shard_map/all_to_all | solution.py:81
  94.8 7.9 %copy-start.1 = (bf16[1,16,2048]{2,1,0:T(8,128)(2,1)S(1)}, bf16[1,16,2048]{2,1,0:T(8,128)(2,1)}, u32[]{:S(2)}) copy-start(bf16[1,16,2048]{2,1,0:T(8,128)(2,1)} %param.10) | copy-start | bytes 196612
  97.1 10.9 %copy-start.2 = (bf16[1,16,2048]{2,1,0:T(8,128)(2,1)S(1)}, bf16[1,16,2048]{2,1,0:T(8,128)(2,1)}, u32[]{:S(2)}) copy-start(bf16[1,16,2048]{2,1,0:T(8,128)(2,1)} %param.11) | copy-start | bytes 196612
  97.1 11.1 %copy-start.3 = (f32[1,2048]{1,0:T(1,128)S(1)}, f32[1,2048]{1,0:T(1,128)}, u32[]{:S(2)}) copy-start(f32[1,2048]{1,0:T(1,128)} %param.12) | copy-start | bytes 24580
  102.7 5.3 %collective-permute-start = (bf16[16,2048]{1,0:T(8,128)(2,1)S(1)}, bf16[16,2048]{1,0:T(8,128)(2,1)S(1)}, u32[]{:S(2)}, u32[]{:S(2)}) collective-permute-start(bf16[16,2048]{1,0:T(8,128)(2,1)S(1)} %fusion.60), channel_id=1, source_target_pairs={{0,16},{1,17},{2,18},{3,19},{4,20},{5,21},{6,22},{7,23},{8,24},{9,... | collective-permute-start | bytes 196616 | tf_op jit(solution)/shard_map/ppermute | solution.py:12
  111.7 29.0 %all-to-all-start.3 = ((bf16[16,9,2048]{2,1,0:T(8,128)(2,1)}), bf16[16,9,2048]{2,1,0:T(8,128)(2,1)}, u32[]{:S(2)}, u32[]{:S(2)}) async-start(bf16[16,9,2048]{2,1,0:T(8,128)(2,1)} %reshape.168), calls=%async_computation.3 | async-start | bytes 2097152 | tf_op jit(solution)/shard_map/all_to_all | solution.py:80
  153.1 29.8 %all-to-all-start.5 = ((bf16[16,9,2048]{2,1,0:T(8,128)(2,1)}), bf16[16,9,2048]{2,1,0:T(8,128)(2,1)}, u32[]{:S(2)}, u32[]{:S(2)}) async-start(bf16[16,9,2048]{2,1,0:T(8,128)(2,1)} %reshape.170), calls=%async_computation.5 | async-start | bytes 2097152 | tf_op jit(solution)/shard_map/all_to_all | solution.py:85
where the time goes:
time: 195 us; the launch traced here: 191 us
  waiting for transfers between devices  92.3 us (47%)
  starting transfers between devices  43.4 us (22%)
  local copies, waits for them, and re-layouts  27.4 us (14%)
  matrix products  18.7 us (10%)
  other arithmetic  9.41 us (5%)
    all_to_all x2, waiting for transfers between devices, local(): lax.all_to_all(outgoing, 'expert', split_axis=0, concat_axis=0, tiled=True)  45.6 us
    all_to_all x2, waiting for transfers between devices, local(): lax.all_to_all(answered, 'expert', split_axis=0, concat_axis=0, tiled=True)  44.9 us
    all_to_all x2, starting transfers between devices, local(): lax.all_to_all(alive_flags, 'expert', split_axis=0, concat_axis=0, tiled=...  14.2 us
    all_to_all x2, starting transfers between devices, local(): lax.all_to_all(answered, 'expert', split_axis=0, concat_axis=0, tiled=True)  13.7 us
    all_to_all x2, starting transfers between devices, local(): lax.all_to_all(outgoing, 'expert', split_axis=0, concat_axis=0, tiled=True)  12.1 us
    dot_general x2, matrix products, swiglu(): jnp.dot(inner, down_matrix, preferred_element_type=jnp.float32)  8.57 us
    dot_general x2, matrix products, swiglu(): jnp.dot(tile_rows, gate_matrix, preferred_element_type=jnp.float32)  6.97 us
    gather x2, local copies, waits for them, and re-layouts, local(): jnp.take(flat_back, target, axis=0)  6.77 us
  transfers between devices with their start and end apart: 7, of which 5 were waited for; matrix products, arithmetic and copies ran while one was open for 10% of the time, Pallas kernels for 0%

commit v1 on v0

v1 whole, which is shorter than its diff:
```python
import functools

import jax
import jax.numpy as jnp
from jax import lax
from jax.experimental import pallas as pl
from jax.experimental.pallas import tpu as pltpu
from jax.sharding import PartitionSpec as P

epsilon = 1e-06
LANES = 128
VMEM = pl.BlockSpec(memory_space=pltpu.VMEM)
SMEM = pl.BlockSpec(memory_space=pltpu.SMEM)


def params(mib):
    return pltpu.CompilerParams(vmem_limit_bytes=mib << 20)


class Plan:
    def __init__(self, size):
        self.size = size
        self.ring = size // 4
        half = self.ring // 2
        pairs = []
        for side in (0, 1):
            for step in range(1, (self.ring + 1) // 2):
                pairs.append(((step, side), (-step, side)))
        if self.ring % 2 == 0:
            pairs.append(((half, 0), (half, 1)))
        self.core = [(i, i ^ 1) for i in range(size)]
        self.side = [(i, i ^ 2) for i in range(size)]
        self.far = [self.mixed(*pair) for pair in pairs]
        self.back = [[(b, a) for a, b in perm] for perm in self.far]

    def mixed(self, first, second):
        out = []
        for i in range(self.size):
            place, side, core = i // 4, (i // 2) % 2, i % 2
            step, flip = (first, second)[core]
            out.append((i, ((place + step) % self.ring) * 4 + (side ^ flip) * 2 + core))
        return out


def rms(values, gain_row):
    scale = lax.rsqrt(jnp.mean(values * values, axis=-1, keepdims=True) + epsilon)
    return (values * scale * gain_row).astype(jnp.bfloat16)


def first_kernel(experts, x_ref, gain_ref, ids_ref, blend_ref, out_ref):
    rows, features = x_ref.shape
    ticks, top = ids_ref.shape[0], ids_ref.shape[2]
    extra = out_ref.shape[1] - features
    out_ref[:, :features] = rms(x_ref[...].astype(jnp.float32), gain_ref[...])
    lane = lax.broadcasted_iota(jnp.int32, (rows, extra), 1)
    expert = lane % experts
    value = jnp.zeros((rows, extra), jnp.float32)
    for tick in range(ticks):
        ids = ids_ref[tick]
        blend = blend_ref[tick]
        mine = lane // (2 * experts) == tick
        for k in range(top):
            hit = jnp.logical_and(mine, expert == ids[:, k : k + 1])
            value = value + jnp.where(hit, blend[:, k : k + 1], 0.0)
    high = value.astype(jnp.bfloat16).astype(jnp.float32)
    low = value - high
    upper = (lane // experts) % 2 == 0
    out_ref[:, features:] = jnp.where(upper, high, low).astype(jnp.bfloat16)


def next_kernel(section_ref, fed_ref, passed_ref, gain_ref, out_ref, state_ref):
    state = jnp.where(section_ref[0] == 0, fed_ref[...].astype(jnp.float32), passed_ref[...].astype(jnp.float32))
    state_ref[...] = state.astype(jnp.bfloat16)
    out_ref[...] = rms(state, gain_ref[...])


def join_kernel(a_ref, b_ref, out_ref):
    rows = a_ref.shape[0]
    out_ref[:rows] = a_ref[...]
    out_ref[rows:] = b_ref[...]


def expert_kernel(tick, experts, pieces, mine_ref, *refs):
    blocks = refs[:pieces]
    refs = refs[pieces:]
    if tick:
        factor_ref, refs = refs[0], refs[1:]
        gate_ref, up_ref, down_ref, keep_ref, send_ref, rows_ref, inner_ref = refs
    else:
        gate_ref, up_ref, down_ref, keep_ref, send_ref, factor_ref, rows_ref, inner_ref = refs
    total, features = rows_ref.shape
    at = 0
    for block in blocks:
        count = block.shape[0]
        rows_ref[at : at + count] = block[:, :features]
        if not tick:
            factor_ref[at : at + count] = block[:, features:]
        at += count
    extra = factor_ref.shape[1]
    hidden = gate_ref.shape[1]
    step = min(256, total)
    wide = 256 if hidden % 256 == 0 else LANES
    tall = 512 if features % 512 == 0 else LANES
    half = total // 2

    @pl.loop(0, total // step)
    def _(part):
        span = pl.ds(pl.multiple_of(part * step, step), step)
        lane = lax.broadcasted_iota(jnp.int32, (step, extra), 1)
        wanted = jnp.logical_and(lane // (2 * experts) == tick, lane % experts == mine_ref[0])
        factor = jnp.sum(jnp.where(wanted, factor_ref[span].astype(jnp.float32), 0.0), axis=1, keepdims=True)
        rows = rows_ref[span]
        for tile in range(hidden // wide):
            cols = slice(tile * wide, (tile + 1) * wide)
            gate = jnp.dot(rows, gate_ref[:, cols], preferred_element_type=jnp.float32)
            up = jnp.dot(rows, up_ref[:, cols], preferred_element_type=jnp.float32)
            inner = gate / (1.0 + jnp.exp(-gate)) * up * factor
            inner_ref[span, cols] = inner.astype(jnp.bfloat16)

    for start, out_ref in ((0, keep_ref), (half, send_ref)):
        inner = inner_ref[start : start + half]
        for tile in range(features // tall):
            cols = slice(tile * tall, (tile + 1) * tall)
            out_ref[:, cols] = jnp.dot(inner, down_ref[:, cols], preferred_element_type=jnp.float32).astype(jnp.bfloat16)


def chip_kernel(keep_ref, got_ref, own_ref, side_ref, *far_refs):
    rows = own_ref.shape[0]
    total = keep_ref[...].astype(jnp.float32) + got_ref[...].astype(jnp.float32)
    own_ref[...] = total[:rows]
    side_ref[...] = total[rows : 2 * rows].astype(jnp.bfloat16)
    for j, far_ref in enumerate(far_refs):
        far_ref[...] = total[2 * rows * (j + 1) : 2 * rows * (j + 2)].astype(jnp.bfloat16)


def gather_kernel(count, x_ref, own_ref, side_ref, *refs):
    far_refs, (mine_ref, other_ref) = refs[:count], refs[count:]
    rows = x_ref.shape[0]
    total = far_refs[0][...].astype(jnp.float32)
    for far_ref in far_refs[1:]:
        total = total + far_ref[...].astype(jnp.float32)
    mine_ref[...] = x_ref[...].astype(jnp.float32) + own_ref[...] + side_ref[...].astype(jnp.float32) + total[:rows]
    other_ref[...] = total[rows:].astype(jnp.bfloat16)


def finish_kernel(mine_ref, got_ref, out_ref):
    out_ref[...] = (mine_ref[...] + got_ref[...].astype(jnp.float32)).astype(jnp.bfloat16)


def last_kernel(mine_ref, got_ref, *refs):
    earlier, out_ref = refs[:-1], refs[-1]
    for tick, ref in enumerate(earlier):
        out_ref[tick, 0] = ref[...]
    out_ref[len(earlier), 0] = (mine_ref[...] + got_ref[...].astype(jnp.float32)).astype(jnp.bfloat16)


def call(kernel, outs, *args, smem=0, scratch=(), mib=32):
    single = not isinstance(outs, (list, tuple))
    return pl.pallas_call(
        kernel,
        out_shape=outs,
        in_specs=[SMEM] * smem + [VMEM] * (len(args) - smem),
        out_specs=VMEM if single else [VMEM] * len(outs),
        scratch_shapes=list(scratch),
        compiler_params=params(mib),
    )(*args)


def shape(rows, columns, dtype=jnp.bfloat16):
    return jax.ShapeDtypeStruct((rows, columns), dtype)


def local(
    resident_batchlets,
    incoming_batchlets,
    segment_rms_gain,
    gating_projection,
    expanding_projection,
    contracting_projection,
    picked_specialist_ids,
    blend_factors,
):
    experts = lax.axis_size("expert")
    sections = lax.axis_size("pipe")
    plan = Plan(experts)
    mine = lax.axis_index("expert").astype(jnp.int32).reshape(1)
    section = lax.axis_index("pipe").astype(jnp.int32).reshape(1)
    rows, features = resident_batchlets.shape[1:]
    ticks = picked_specialist_ids.shape[0]
    extra = -(-2 * ticks * experts // LANES) * LANES
    weights = (gating_projection[0], expanding_projection[0], contracting_projection[0])
    hidden = weights[0].shape[1]
    total = rows * experts

    def move(value, perm):
        return lax.ppermute(value, "expert", perm)

    state = resident_batchlets[0]
    factors = None
    outputs = []
    for tick in range(ticks):
        if tick == 0:
            normed = call(
                functools.partial(first_kernel, experts),
                shape(rows, features + extra),
                state,
                segment_rms_gain,
                picked_specialist_ids[:, 0],
                blend_factors[:, 0],
            )
        else:
            passed = lax.ppermute(outputs[-1], "pipe", [(i, i + 1) for i in range(sections - 1)])
            normed, state = call(
                next_kernel,
                [shape(rows, features), shape(rows, features)],
                section,
                incoming_batchlets[tick - 1],
                passed,
                segment_rms_gain,
                smem=1,
            )
        width = normed.shape[1]
        beside = move(normed, plan.side)
        partner = move(normed, plan.core)
        chip = call(join_kernel, shape(2 * rows, width), normed, partner)
        far = [move(chip, perm) for perm in plan.far]
        direct = [normed, beside] + far
        relayed = [partner] + [move(block, plan.core) for block in direct[1:]]
        blocks = direct + relayed
        outs = [shape(total // 2, features), shape(total // 2, features)]
        if tick == 0:
            outs.append(shape(total, extra))
        args = [mine] + blocks + ([factors] if tick else []) + list(weights)
        got = call(
            functools.partial(expert_kernel, tick, experts, len(blocks)),
            outs,
            *args,
            smem=1,
            scratch=[pltpu.VMEM((total, features), jnp.bfloat16), pltpu.VMEM((total, hidden), jnp.bfloat16)],
            mib=48,
        )
        keep, send = got[:2]
        if tick == 0:
            factors = got[2]
        swapped = move(send, plan.core)
        own, side, *far = call(
            chip_kernel,
            [shape(rows, features, jnp.float32), shape(rows, features)] + [shape(2 * rows, features)] * len(plan.back),
            keep,
            swapped,
        )
        far = [move(block, perm) for block, perm in zip(far, plan.back)]
        side = move(side, plan.side)
        part, other = call(
            functools.partial(gather_kernel, len(far)),
            [shape(rows, features, jnp.float32), shape(rows, features)],
            state,
            own,
            side,
            *far,
        )
        other = move(other, plan.core)
        if tick + 1 < ticks:
            outputs.append(call(finish_kernel, shape(rows, features), part, other))
        else:
            return call(last_kernel, jax.ShapeDtypeStruct((ticks, 1, rows, features), jnp.bfloat16), part, other, *outputs)


def solution(mesh):
    in_specs = (
        P("pipe", "expert", None),
        P(None, "expert", None),
        P("pipe", None),
        P("expert", None, None),
        P("expert", None, None),
        P("expert", None, None),
        P(None, "pipe", "expert", None),
        P(None, "pipe", "expert", None),
    )
    out_specs = P(None, "pipe", "expert", None)
    return jax.shard_map(local, mesh=mesh, in_specs=in_specs, out_specs=out_specs, check_vma=False)
```

time: 195 us -> 108 us (0.55); the launches traced: 191 us -> 107 us
  waiting for transfers between devices: 92.3 us -> 45.8 us
  matrix products: 18.7 us -> 0 us
  Pallas kernels: 0 us -> 12.6 us
  local copies, waits for them, and re-layouts: 27.4 us -> 16 us
  starting transfers between devices: 43.4 us -> 32.5 us
  other arithmetic: 9.41 us -> 0 us
    all_to_all x6 -> x0, waiting for transfers between devices: 90.5 us -> none  [the longest x2 45.6 us: local(): lax.all_to_all(outgoing, 'expert', split_axis=0, concat_axis=0, tiled=True)]
    ppermute x1 -> x31, waiting for transfers between devices: 1.78 us -> 45.8 us  [the longest x30 43.9 us: move(): return lax.ppermute(value, 'expert', perm)]
    all_to_all x6 -> x0, starting transfers between devices: 40 us -> none  [the longest x2 14.2 us: local(): lax.all_to_all(alive_flags, 'expert', split_axis=0, concat_axis=0, tiled=...]
    ppermute x1 -> x31, starting transfers between devices: 3.42 us -> 32.5 us  [the longest x30 29.1 us: move(): return lax.ppermute(value, 'expert', perm)]
    dot_general x6 -> x0, matrix products: 18.7 us -> none  [the longest x2 8.57 us: swiglu(): jnp.dot(inner, down_matrix, preferred_element_type=jnp.float32)]
    reshape x8 -> x0, local copies, waits for them, and re-layouts: 18.6 us -> none  [the longest x2 4.68 us: expert_rows(): return result.reshape(sources, item_count, feature_count)]
    unnamed x10 -> x44, local copies, waits for them, and re-layouts: 0.02 us -> 16 us
    pallas_call x0 -> x12, Pallas kernels: none -> 12.6 us  [call(): pl.pallas_call(kernel, out_shape=outs, in_specs=[SMEM] * smem + [VMEM] *...]
  transfers between devices with their start and end apart: 7 -> 31, of which waited for: 5 -> 17; matrix products, arithmetic and copies ran while one was open for 10% -> 0% of each run, Pallas kernels for 0% -> 0%
where the time goes in v1:
time: 108 us; the launch traced here: 107 us
  waiting for transfers between devices  45.8 us (42%)
  starting transfers between devices  32.5 us (30%)
  local copies, waits for them, and re-layouts  16 us (15%)
  Pallas kernels  12.6 us (12%)
    ppermute x30, waiting for transfers between devices, move(): return lax.ppermute(value, 'expert', perm)  43.9 us
    ppermute x30, starting transfers between devices, move(): return lax.ppermute(value, 'expert', perm)  29.1 us
    unnamed x44, local copies, waits for them, and re-layouts  16 us
    pallas_call x12, Pallas kernels, call(): pl.pallas_call(kernel, out_shape=outs, in_specs=[SMEM] * smem + [VMEM] *...  12.6 us
    ppermute x1, starting transfers between devices, local(): lax.ppermute(outputs[-1], 'pipe', [(i, i + 1) for i in range(sections - 1)])  3.42 us
  transfers between devices with their start and end apart: 31, of which 17 were waited for; matrix products, arithmetic and copies ran while one was open for 0% of the time, Pallas kernels for 0%

profile of v1, /device:TPU:0, one launch (start us, length us, event | category | flops | bytes accessed | tf_op | source)
XLA Modules:
  0.0 107.0 jit_solution(15045632205642404800)
XLA Ops:
  0.0 0.8 copy.9
  0.8 0.8 copy.10
  1.5 0.8 copy-done.2
  2.4 0.7 copy-done.19
  3.1 0.2 shard_map.82.a_ref.refs_0_
  3.3 0.6 collective-permute-start.1
  3.8 0.9 collective-permute-done.1.b_ref.refs_5_
  4.7 4.0 %collective-permute-start.4 = (bf16[32,2176]{1,0:T(8,128)(2,1)S(1)}, bf16[32,2176]{1,0:T(8,128)(2,1)S(1)}, u32[]{:S(2)}, u32[]{:S(2)}) collective-permute-start(bf16[32,2176]{1,0:T(8,128)(2,1)S(1)} %shard_map.83), channel_id=1, source_target_pairs={{0,8},{1,11},{2,10},{3,9},{4,12},{5,15},{6,14},{7,13},{8,0},{9,3},... | collective-permute-start | bytes 417800 | tf_op jit(solution)/shard_map/ppermute | solution.py:196
  8.7 2.5 %collective-permute-start.3 = (bf16[32,2176]{1,0:T(8,128)(2,1)S(1)}, bf16[32,2176]{1,0:T(8,128)(2,1)S(1)}, u32[]{:S(2)}, u32[]{:S(2)}) collective-permute-start(bf16[32,2176]{1,0:T(8,128)(2,1)S(1)} %shard_map.83), channel_id=1, source_target_pairs={{0,6},{1,15},{2,4},{3,13},{4,10},{5,3},{6,8},{7,1},{8,14},{9,7},{1... | collective-permute-start | bytes 417800 | tf_op jit(solution)/shard_map/ppermute | solution.py:196
  11.2 0.6 collective-permute-start
  11.8 4.9 %collective-permute-done.4.refs_4_ = bf16[32,2176]{1,0:T(8,128)(2,1)S(1)} collective-permute-done((bf16[32,2176]{1,0:T(8,128)(2,1)S(1)}, bf16[32,2176]{1,0:T(8,128)(2,1)S(1)}, u32[]{:S(2)}, u32[]{:S(2)}) %collective-permute-start.4) | collective-permute-done | bytes 139296 | tf_op jit(solution)/shard_map/ppermute | solution.py:196
  16.7 1.8 %collective-permute-done.3.refs_3_ = bf16[32,2176]{1,0:T(8,128)(2,1)S(1)} collective-permute-done((bf16[32,2176]{1,0:T(8,128)(2,1)S(1)}, bf16[32,2176]{1,0:T(8,128)(2,1)S(1)}, u32[]{:S(2)}, u32[]{:S(2)}) %collective-permute-start.3) | collective-permute-done | bytes 139296 | tf_op jit(solution)/shard_map/ppermute | solution.py:196
  18.6 0.7 copy-done.4
  19.2 1.4 %collective-permute-done.2.refs_2_ = bf16[32,2176]{1,0:T(8,128)(2,1)S(1)} collective-permute-done((bf16[32,2176]{1,0:T(8,128)(2,1)S(1)}, bf16[32,2176]{1,0:T(8,128)(2,1)S(1)}, u32[]{:S(2)}, u32[]{:S(2)}) %collective-permute-start.2) | collective-permute-done | bytes 139296 | tf_op jit(solution)/shard_map/ppermute | solution.py:196
  20.6 0.7 copy-done.6
  21.3 0.5 collective-permute-start.5
  21.8 0.9 collective-permute-done.5.refs_6_
  22.7 0.6 copy-done.14
  23.3 0.7 copy-done.8
  24.0 0.7 copy-done.10
  24.7 0.6 copy-done.12
  25.3 1.9 %copy-done = bf16[1,2048,768]{2,1,0:T(8,128)(2,1)S(1)} copy-done((bf16[1,2048,768]{2,1,0:T(8,128)(2,1)S(1)}, bf16[1,2048,768]{2,1,0:T(8,128)(2,1)}, u32[]{:S(2)}) %copy-start) | copy-done | bytes 3145752
  27.2 0.9 copy-done.5
  28.1 0.9 copy-done.7
  29.0 0.9 copy-done.9
  29.9 0.9 copy-done.11
  30.8 0.9 copy-done.13
  31.7 0.9 copy-done.15
  32.6 5.7 %shard_map.84 = (bf16[128,2048]{1,0:T(8,128)(2,1)S(1)}, bf16[128,2048]{1,0:T(8,128)(2,1)S(1)}, bf16[256,128]{1,0:T(8,128)(2,1)S(1)}) custom-call(s32[1]{0:T(128)} %bitcast.3.mine_ref, bf16[16,2176]{1,0:T(8,128)(2,1)S(1)} %shard_map.82.a_ref.refs_0_, bf16[16,2176]{1,0:T(8,128)(2,1)S(1)} %collective-permute-done.refs_1_, bf16[32,2176]{1,0:T(8,128)(2,1)S(1)} %copy-done.7, ...), custom_call_target="tpu_custom_call" | custom-call | tf_op jit(solution)/shard_map/pallas_call | solution.py:159
  38.3 0.4 collective-permute-start.9
  38.8 1.6 %collective-permute-done.9.got_ref = bf16[128,2048]{1,0:T(8,128)(2,1)S(1)} collective-permute-done((bf16[128,2048]{1,0:T(8,128)(2,1)S(1)}, bf16[128,2048]{1,0:T(8,128)(2,1)S(1)}, u32[]{:S(2)}, u32[]{:S(2)}) %collective-permute-start.9) | collective-permute-done | bytes 524320 | tf_op jit(solution)/shard_map/ppermute | solution.py:196
  40.3 0.1 shard_map.85
  40.4 3.8 %collective-permute-start.11 = (bf16[32,2048]{1,0:T(8,128)(2,1)S(1)}, bf16[32,2048]{1,0:T(8,128)(2,1)S(1)}, u32[]{:S(2)}, u32[]{:S(2)}) collective-permute-start(bf16[32,2048]{1,0:T(8,128)(2,1)S(1)} %get-tuple-element.30), channel_id=1, source_target_pairs={{4,0},{13,1},{6,2},{15,3},{8,4},{1,5},{10,6},{3,7},{12,8},{5,9},{1... | collective-permute-start | bytes 393224 | tf_op jit(solution)/shard_map/ppermute | solution.py:196
  44.3 2.7 %collective-permute-start.12 = (bf16[32,2048]{1,0:T(8,128)(2,1)S(1)}, bf16[32,2048]{1,0:T(8,128)(2,1)S(1)}, u32[]{:S(2)}, u32[]{:S(2)}) collective-permute-start(bf16[32,2048]{1,0:T(8,128)(2,1)S(1)} %get-tuple-element.31), channel_id=1, source_target_pairs={{6,0},{15,1},{4,2},{13,3},{10,4},{3,5},{8,6},{1,7},{14,8},{7,9},{1... | collective-permute-start | bytes 393224 | tf_op jit(solution)/shard_map/ppermute | solution.py:196
  46.9 1.0 collective-permute-start.10
  48.0 5.3 %collective-permute-done.10.side_ref = bf16[16,2048]{1,0:T(8,128)(2,1)S(1)} collective-permute-done((bf16[16,2048]{1,0:T(8,128)(2,1)S(1)}, bf16[16,2048]{1,0:T(8,128)(2,1)S(1)}, u32[]{:S(2)}, u32[]{:S(2)}) %collective-permute-start.10) | collective-permute-done | bytes 65568 | tf_op jit(solution)/shard_map/ppermute | solution.py:196
  53.3 3.5 %collective-permute-done.13.refs_2_ = bf16[32,2048]{1,0:T(8,128)(2,1)S(1)} collective-permute-done((bf16[32,2048]{1,0:T(8,128)(2,1)S(1)}, bf16[32,2048]{1,0:T(8,128)(2,1)S(1)}, u32[]{:S(2)}, u32[]{:S(2)}) %collective-permute-start.13) | collective-permute-done | bytes 131104 | tf_op jit(solution)/shard_map/ppermute | solution.py:196
  56.8 0.1 collective-permute-start.14
  56.9 1.2 %collective-permute-done.14.got_ref = bf16[16,2048]{1,0:T(8,128)(2,1)S(1)} collective-permute-done((bf16[16,2048]{1,0:T(8,128)(2,1)S(1)}, bf16[16,2048]{1,0:T(8,128)(2,1)S(1)}, u32[]{:S(2)}, u32[]{:S(2)}) %collective-permute-start.14) | collective-permute-done | bytes 65568 | tf_op jit(solution)/shard_map/ppermute | solution.py:196
  58.2 3.4 %collective-permute-start.15 = (bf16[16,2048]{1,0:T(8,128)(2,1)S(1)}, bf16[16,2048]{1,0:T(8,128)(2,1)S(1)}, u32[]{:S(2)}, u32[]{:S(2)}) collective-permute-start(bf16[16,2048]{1,0:T(8,128)(2,1)S(1)} %shard_map.87.refs_0_), channel_id=1, source_target_pairs={{0,16},{1,17},{2,18},{3,19},{4,20},{5,21},{6,22},{7,23},{8,24},{9,... | collective-permute-start | bytes 196616 | tf_op jit(solution)/shard_map/ppermute | solution.py:212
  61.6 1.9 %collective-permute-done.15.passed_ref = bf16[16,2048]{1,0:T(8,128)(2,1)S(1)} collective-permute-done((bf16[16,2048]{1,0:T(8,128)(2,1)S(1)}, bf16[16,2048]{1,0:T(8,128)(2,1)S(1)}, u32[]{:S(2)}, u32[]{:S(2)}) %collective-permute-start.15) | collective-permute-done | bytes 65568 | tf_op jit(solution)/shard_map/ppermute | solution.py:212
  63.5 0.8 copy-done.18
  64.4 0.1 shard_map.88
  64.6 1.2 %collective-permute-done.17.b_ref.refs_5_ = bf16[16,2048]{1,0:T(8,128)(2,1)S(1)} collective-permute-done((bf16[16,2048]{1,0:T(8,128)(2,1)S(1)}, bf16[16,2048]{1,0:T(8,128)(2,1)S(1)}, u32[]{:S(2)}, u32[]{:S(2)}) %collective-permute-start.17) | collective-permute-done | bytes 65568 | tf_op jit(solution)/shard_map/ppermute | solution.py:196
  65.8 0.7 collective-permute-start.20
  66.6 3.6 %collective-permute-start.19 = (bf16[32,2048]{1,0:T(8,128)(2,1)S(1)}, bf16[32,2048]{1,0:T(8,128)(2,1)S(1)}, u32[]{:S(2)}, u32[]{:S(2)}) collective-permute-start(bf16[32,2048]{1,0:T(8,128)(2,1)S(1)} %shard_map.89), channel_id=1, source_target_pairs={{0,6},{1,15},{2,4},{3,13},{4,10},{5,3},{6,8},{7,1},{8,14},{9,7},{1... | collective-permute-start | bytes 393224 | tf_op jit(solution)/shard_map/ppermute | solution.py:196
  70.2 0.8 collective-permute-start.16
  71.0 7.5 %collective-permute-done.20.refs_4_ = bf16[32,2048]{1,0:T(8,128)(2,1)S(1)} collective-permute-done((bf16[32,2048]{1,0:T(8,128)(2,1)S(1)}, bf16[32,2048]{1,0:T(8,128)(2,1)S(1)}, u32[]{:S(2)}, u32[]{:S(2)}) %collective-permute-start.20) | collective-permute-done | bytes 131104 | tf_op jit(solution)/shard_map/ppermute | solution.py:196
  78.5 0.5 collective-permute-start.23
  79.1 0.4 collective-permute-start.21
  79.5 0.9 collective-permute-done.21.refs_6_
  80.5 0.8 copy-done.17
  81.3 5.5 %shard_map.90 = (bf16[128,2048]{1,0:T(8,128)(2,1)S(1)}, bf16[128,2048]{1,0:T(8,128)(2,1)S(1)}) custom-call(s32[1]{0:T(128)} %bitcast.3.mine_ref, bf16[16,2048]{1,0:T(8,128)(2,1)S(1)} %get-tuple-element.36.a_ref.refs_0_, bf16[16,2048]{1,0:T(8,128)(2,1)S(1)} %collective-permute-done.16.refs_1_, bf16[32,2048]{1,0:T(8,128)(2,1)S(1)} %collective-permute-done.18.refs_2_, ...), custom_call_target="tpu_custom_call" | custom-call | tf_op jit(solution)/shard_map/pallas_call | solution.py:159
  86.8 0.4 collective-permute-start.25
  87.2 1.6 %collective-permute-done.25.got_ref = bf16[128,2048]{1,0:T(8,128)(2,1)S(1)} collective-permute-done((bf16[128,2048]{1,0:T(8,128)(2,1)S(1)}, bf16[128,2048]{1,0:T(8,128)(2,1)S(1)}, u32[]{:S(2)}, u32[]{:S(2)}) %collective-permute-start.25) | collective-permute-done | bytes 524320 | tf_op jit(solution)/shard_map/ppermute | solution.py:196
  88.8 0.1 shard_map.91
  88.9 2.7 %collective-permute-start.27 = (bf16[32,2048]{1,0:T(8,128)(2,1)S(1)}, bf16[32,2048]{1,0:T(8,128)(2,1)S(1)}, u32[]{:S(2)}, u32[]{:S(2)}) collective-permute-start(bf16[32,2048]{1,0:T(8,128)(2,1)S(1)} %get-tuple-element.42), channel_id=1, source_target_pairs={{4,0},{13,1},{6,2},{15,3},{8,4},{1,5},{10,6},{3,7},{12,8},{5,9},{1... | collective-permute-start | bytes 393224 | tf_op jit(solution)/shard_map/ppermute | solution.py:196
  91.6 2.2 %collective-permute-start.28 = (bf16[32,2048]{1,0:T(8,128)(2,1)S(1)}, bf16[32,2048]{1,0:T(8,128)(2,1)S(1)}, u32[]{:S(2)}, u32[]{:S(2)}) collective-permute-start(bf16[32,2048]{1,0:T(8,128)(2,1)S(1)} %get-tuple-element.43), channel_id=1, source_target_pairs={{6,0},{15,1},{4,2},{13,3},{10,4},{3,5},{8,6},{1,7},{14,8},{7,9},{1... | collective-permute-start | bytes 393224 | tf_op jit(solution)/shard_map/ppermute | solution.py:196
  93.8 1.3 %collective-permute-start.26 = (bf16[16,2048]{1,0:T(8,128)(2,1)S(1)}, bf16[16,2048]{1,0:T(8,128)(2,1)S(1)}, u32[]{:S(2)}, u32[]{:S(2)}) collective-permute-start(bf16[16,2048]{1,0:T(8,128)(2,1)S(1)} %get-tuple-element.41), channel_id=1, source_target_pairs={{0,2},{1,3},{2,0},{3,1},{4,6},{5,7},{6,4},{7,5},{8,10},{9,11},{10,... | collective-permute-start | bytes 196616 | tf_op jit(solution)/shard_map/ppermute | solution.py:196
  95.1 6.1 %collective-permute-done.26.side_ref = bf16[16,2048]{1,0:T(8,128)(2,1)S(1)} collective-permute-done((bf16[16,2048]{1,0:T(8,128)(2,1)S(1)}, bf16[16,2048]{1,0:T(8,128)(2,1)S(1)}, u32[]{:S(2)}, u32[]{:S(2)}) %collective-permute-start.26) | collective-permute-done | bytes 65568 | tf_op jit(solution)/shard_map/ppermute | solution.py:196
  101.2 3.8 %collective-permute-done.29.refs_2_ = bf16[32,2048]{1,0:T(8,128)(2,1)S(1)} collective-permute-done((bf16[32,2048]{1,0:T(8,128)(2,1)S(1)}, bf16[32,2048]{1,0:T(8,128)(2,1)S(1)}, u32[]{:S(2)}, u32[]{:S(2)}) %collective-permute-start.29) | collective-permute-done | bytes 131104 | tf_op jit(solution)/shard_map/ppermute | solution.py:196
  105.0 0.1 collective-permute-start.30
  105.1 1.2 %collective-permute-done.30.got_ref = bf16[16,2048]{1,0:T(8,128)(2,1)S(1)} collective-permute-done((bf16[16,2048]{1,0:T(8,128)(2,1)S(1)}, bf16[16,2048]{1,0:T(8,128)(2,1)S(1)}, u32[]{:S(2)}, u32[]{:S(2)}) %collective-permute-start.30) | collective-permute-done | bytes 65568 | tf_op jit(solution)/shard_map/ppermute | solution.py:196
  106.3 0.7 shard_map.93
  (54 shorter events, 0.4 us)
Async XLA Ops:
  1.5 0.8 copy-start.2
  2.4 0.7 copy-start.19
  3.3 1.5 %collective-permute-start.1 = (bf16[16,2176]{1,0:T(8,128)(2,1)S(1)}, bf16[16,2176]{1,0:T(8,128)(2,1)S(1)}, u32[]{:S(2)}, u32[]{:S(2)}) collective-permute-start(bf16[16,2176]{1,0:T(8,128)(2,1)S(1)} %shard_map.82.a_ref.refs_0_), channel_id=1, source_target_pairs={{0,1},{1,0},{2,3},{3,2},{4,5},{5,4},{6,7},{7,6},{8,9},{9,8},{10,11... | collective-permute-start | bytes 208904 | tf_op jit(solution)/shard_map/ppermute | solution.py:196
  4.7 12.0 %collective-permute-start.4 = (bf16[32,2176]{1,0:T(8,128)(2,1)S(1)}, bf16[32,2176]{1,0:T(8,128)(2,1)S(1)}, u32[]{:S(2)}, u32[]{:S(2)}) collective-permute-start(bf16[32,2176]{1,0:T(8,128)(2,1)S(1)} %shard_map.83), channel_id=1, source_target_pairs={{0,8},{1,11},{2,10},{3,9},{4,12},{5,15},{6,14},{7,13},{8,0},{9,3},... | collective-permute-start | bytes 417800 | tf_op jit(solution)/shard_map/ppermute | solution.py:196
  8.7 9.8 %collective-permute-start.3 = (bf16[32,2176]{1,0:T(8,128)(2,1)S(1)}, bf16[32,2176]{1,0:T(8,128)(2,1)S(1)}, u32[]{:S(2)}, u32[]{:S(2)}) collective-permute-start(bf16[32,2176]{1,0:T(8,128)(2,1)S(1)} %shard_map.83), channel_id=1, source_target_pairs={{0,6},{1,15},{2,4},{3,13},{4,10},{5,3},{6,8},{7,1},{8,14},{9,7},{1... | collective-permute-start | bytes 417800 | tf_op jit(solution)/shard_map/ppermute | solution.py:196
  11.2 9.4 %collective-permute-start.2 = (bf16[32,2176]{1,0:T(8,128)(2,1)S(1)}, bf16[32,2176]{1,0:T(8,128)(2,1)S(1)}, u32[]{:S(2)}, u32[]{:S(2)}) collective-permute-start(bf16[32,2176]{1,0:T(8,128)(2,1)S(1)} %shard_map.83), channel_id=1, source_target_pairs={{0,4},{1,13},{2,6},{3,15},{4,8},{5,1},{6,10},{7,3},{8,12},{9,5},{1... | collective-permute-start | bytes 417800 | tf_op jit(solution)/shard_map/ppermute | solution.py:196
  11.2 10.1 %collective-permute-start = (bf16[16,2176]{1,0:T(8,128)(2,1)S(1)}, bf16[16,2176]{1,0:T(8,128)(2,1)S(1)}, u32[]{:S(2)}, u32[]{:S(2)}) collective-permute-start(bf16[16,2176]{1,0:T(8,128)(2,1)S(1)} %shard_map.82.a_ref.refs_0_), channel_id=1, source_target_pairs={{0,2},{1,3},{2,0},{3,1},{4,6},{5,7},{6,4},{7,5},{8,10},{9,11},{10,... | collective-permute-start | bytes 208904 | tf_op jit(solution)/shard_map/ppermute | solution.py:196
  16.7 6.6 %collective-permute-start.8 = (bf16[32,2176]{1,0:T(8,128)(2,1)S(1)}, bf16[32,2176]{1,0:T(8,128)(2,1)S(1)}, u32[]{:S(2)}, u32[]{:S(2)}) collective-permute-start(bf16[32,2176]{1,0:T(8,128)(2,1)S(1)} %collective-permute-done.4.refs_4_), channel_id=1, source_target_pairs={{0,1},{1,0},{2,3},{3,2},{4,5},{5,4},{6,7},{7,6},{8,9},{9,8},{10,11... | collective-permute-start | bytes 417800 | tf_op jit(solution)/shard_map/ppermute | solution.py:196
  18.6 5.4 %collective-permute-start.7 = (bf16[32,2176]{1,0:T(8,128)(2,1)S(1)}, bf16[32,2176]{1,0:T(8,128)(2,1)S(1)}, u32[]{:S(2)}, u32[]{:S(2)}) collective-permute-start(bf16[32,2176]{1,0:T(8,128)(2,1)S(1)} %collective-permute-done.3.refs_3_), channel_id=1, source_target_pairs={{0,1},{1,0},{2,3},{3,2},{4,5},{5,4},{6,7},{7,6},{8,9},{9,8},{10,11... | collective-permute-start | bytes 417800 | tf_op jit(solution)/shard_map/ppermute | solution.py:196
  18.6 0.7 copy-start.4
  20.6 4.0 %collective-permute-start.6 = (bf16[32,2176]{1,0:T(8,128)(2,1)S(1)}, bf16[32,2176]{1,0:T(8,128)(2,1)S(1)}, u32[]{:S(2)}, u32[]{:S(2)}) collective-permute-start(bf16[32,2176]{1,0:T(8,128)(2,1)S(1)} %collective-permute-done.2.refs_2_), channel_id=1, source_target_pairs={{0,1},{1,0},{2,3},{3,2},{4,5},{5,4},{6,7},{7,6},{8,9},{9,8},{10,11... | collective-permute-start | bytes 417800 | tf_op jit(solution)/shard_map/ppermute | solution.py:196
  20.6 0.7 copy-start.6
  21.3 1.4 %collective-permute-start.5 = (bf16[16,2176]{1,0:T(8,128)(2,1)S(1)}, bf16[16,2176]{1,0:T(8,128)(2,1)S(1)}, u32[]{:S(2)}, u32[]{:S(2)}) collective-permute-start(bf16[16,2176]{1,0:T(8,128)(2,1)S(1)} %collective-permute-done.refs_1_), channel_id=1, source_target_pairs={{0,1},{1,0},{2,3},{3,2},{4,5},{5,4},{6,7},{7,6},{8,9},{9,8},{10,11... | collective-permute-start | bytes 208904 | tf_op jit(solution)/shard_map/ppermute | solution.py:196
  22.7 0.6 copy-start.14
  23.3 0.7 copy-start.8
  24.0 0.7 copy-start.10
  24.6 0.6 copy-start.12
  25.3 1.9 %copy-start = (bf16[1,2048,768]{2,1,0:T(8,128)(2,1)S(1)}, bf16[1,2048,768]{2,1,0:T(8,128)(2,1)}, u32[]{:S(2)}) copy-start(bf16[1,2048,768]{2,1,0:T(8,128)(2,1)} %param.11) | copy-start | bytes 9437188
  27.2 0.9 copy-start.5
  28.1 0.9 copy-start.7
  29.0 0.9 copy-start.9
  29.9 0.9 copy-start.11
  30.8 0.9 copy-start.13
  31.7 0.9 copy-start.15
  32.6 24.2 %copy-start.3 = (bf16[1,16,2048]{2,1,0:T(8,128)(2,1)S(1)}, bf16[1,16,2048]{2,1,0:T(8,128)(2,1)}, u32[]{:S(2)}) copy-start(bf16[1,16,2048]{2,1,0:T(8,128)(2,1)} %param.8) | copy-start | bytes 196612
  32.6 30.9 %copy-start.20 = (f32[1,2048]{1,0:T(1,128)S(1)}, f32[1,2048]{1,0:T(1,128)}, u32[]{:S(2)}) copy-start(f32[1,2048]{1,0:T(1,128)} %gain_ref.3) | copy-start | bytes 24580
  32.6 47.9 %copy-start.1 = (bf16[1,2048,768]{2,1,0:T(8,128)(2,1)S(1)}, bf16[1,2048,768]{2,1,0:T(8,128)(2,1)}, u32[]{:S(2)}) copy-start(bf16[1,2048,768]{2,1,0:T(8,128)(2,1)} %param.11) | copy-start | bytes 9437188
  38.3 19.9 %copy-start.16 = (bf16[256,128]{1,0:T(8,128)(2,1)}, bf16[256,128]{1,0:T(8,128)(2,1)S(1)}, u32[]{:S(2)}) copy-start(bf16[256,128]{1,0:T(8,128)(2,1)S(1)} %get-tuple-element.37.refs_10_) | copy-start | bytes 196612
  38.3 2.0 %collective-permute-start.9 = (bf16[128,2048]{1,0:T(8,128)(2,1)S(1)}, bf16[128,2048]{1,0:T(8,128)(2,1)S(1)}, u32[]{:S(2)}, u32[]{:S(2)}) collective-permute-start(bf16[128,2048]{1,0:T(8,128)(2,1)S(1)} %get-tuple-element.27), channel_id=1, source_target_pairs={{0,1},{1,0},{2,3},{3,2},{4,5},{5,4},{6,7},{7,6},{8,9},{9,8},{10,11... | collective-permute-start | bytes 1572872 | tf_op jit(solution)/shard_map/ppermute | solution.py:196
  40.4 12.8 %collective-permute-start.11 = (bf16[32,2048]{1,0:T(8,128)(2,1)S(1)}, bf16[32,2048]{1,0:T(8,128)(2,1)S(1)}, u32[]{:S(2)}, u32[]{:S(2)}) collective-permute-start(bf16[32,2048]{1,0:T(8,128)(2,1)S(1)} %get-tuple-element.30), channel_id=1, source_target_pairs={{4,0},{13,1},{6,2},{15,3},{8,4},{1,5},{10,6},{3,7},{12,8},{5,9},{1... | collective-permute-start | bytes 393224 | tf_op jit(solution)/shard_map/ppermute | solution.py:196
  44.3 9.0 %collective-permute-start.12 = (bf16[32,2048]{1,0:T(8,128)(2,1)S(1)}, bf16[32,2048]{1,0:T(8,128)(2,1)S(1)}, u32[]{:S(2)}, u32[]{:S(2)}) collective-permute-start(bf16[32,2048]{1,0:T(8,128)(2,1)S(1)} %get-tuple-element.31), channel_id=1, source_target_pairs={{6,0},{15,1},{4,2},{13,3},{10,4},{3,5},{8,6},{1,7},{14,8},{7,9},{1... | collective-permute-start | bytes 393224 | tf_op jit(solution)/shard_map/ppermute | solution.py:196
  46.9 9.8 %collective-permute-start.13 = (bf16[32,2048]{1,0:T(8,128)(2,1)S(1)}, bf16[32,2048]{1,0:T(8,128)(2,1)S(1)}, u32[]{:S(2)}, u32[]{:S(2)}) collective-permute-start(bf16[32,2048]{1,0:T(8,128)(2,1)S(1)} %get-tuple-element.32), channel_id=1, source_target_pairs={{8,0},{11,1},{10,2},{9,3},{12,4},{15,5},{14,6},{13,7},{0,8},{3,9},... | collective-permute-start | bytes 393224 | tf_op jit(solution)/shard_map/ppermute | solution.py:196
  46.9 6.3 %collective-permute-start.10 = (bf16[16,2048]{1,0:T(8,128)(2,1)S(1)}, bf16[16,2048]{1,0:T(8,128)(2,1)S(1)}, u32[]{:S(2)}, u32[]{:S(2)}) collective-permute-start(bf16[16,2048]{1,0:T(8,128)(2,1)S(1)} %get-tuple-element.29), channel_id=1, source_target_pairs={{0,2},{1,3},{2,0},{3,1},{4,6},{5,7},{6,4},{7,5},{8,10},{9,11},{10,... | collective-permute-start | bytes 196616 | tf_op jit(solution)/shard_map/ppermute | solution.py:196
  56.8 1.3 %collective-permute-start.14 = (bf16[16,2048]{1,0:T(8,128)(2,1)S(1)}, bf16[16,2048]{1,0:T(8,128)(2,1)S(1)}, u32[]{:S(2)}, u32[]{:S(2)}) collective-permute-start(bf16[16,2048]{1,0:T(8,128)(2,1)S(1)} %get-tuple-element.34), channel_id=1, source_target_pairs={{0,1},{1,0},{2,3},{3,2},{4,5},{5,4},{6,7},{7,6},{8,9},{9,8},{10,11... | collective-permute-start | bytes 196616 | tf_op jit(solution)/shard_map/ppermute | solution.py:196
  58.2 5.3 %collective-permute-start.15 = (bf16[16,2048]{1,0:T(8,128)(2,1)S(1)}, bf16[16,2048]{1,0:T(8,128)(2,1)S(1)}, u32[]{:S(2)}, u32[]{:S(2)}) collective-permute-start(bf16[16,2048]{1,0:T(8,128)(2,1)S(1)} %shard_map.87.refs_0_), channel_id=1, source_target_pairs={{0,16},{1,17},{2,18},{3,19},{4,20},{5,21},{6,22},{7,23},{8,24},{9,... | collective-permute-start | bytes 196616 | tf_op jit(solution)/shard_map/ppermute | solution.py:212
  63.5 0.8 copy-start.18
  64.5 1.3 %collective-permute-start.17 = (bf16[16,2048]{1,0:T(8,128)(2,1)S(1)}, bf16[16,2048]{1,0:T(8,128)(2,1)S(1)}, u32[]{:S(2)}, u32[]{:S(2)}) collective-permute-start(bf16[16,2048]{1,0:T(8,128)(2,1)S(1)} %get-tuple-element.36.a_ref.refs_0_), channel_id=1, source_target_pairs={{0,1},{1,0},{2,3},{3,2},{4,5},{5,4},{6,7},{7,6},{8,9},{9,8},{10,11... | collective-permute-start | bytes 196616 | tf_op jit(solution)/shard_map/ppermute | solution.py:196
  65.8 12.7 %collective-permute-start.20 = (bf16[32,2048]{1,0:T(8,128)(2,1)S(1)}, bf16[32,2048]{1,0:T(8,128)(2,1)S(1)}, u32[]{:S(2)}, u32[]{:S(2)}) collective-permute-start(bf16[32,2048]{1,0:T(8,128)(2,1)S(1)} %shard_map.89), channel_id=1, source_target_pairs={{0,8},{1,11},{2,10},{3,9},{4,12},{5,15},{6,14},{7,13},{8,0},{9,3},... | collective-permute-start | bytes 393224 | tf_op jit(solution)/shard_map/ppermute | solution.py:196
  66.6 12.0 %collective-permute-start.19 = (bf16[32,2048]{1,0:T(8,128)(2,1)S(1)}, bf16[32,2048]{1,0:T(8,128)(2,1)S(1)}, u32[]{:S(2)}, u32[]{:S(2)}) collective-permute-start(bf16[32,2048]{1,0:T(8,128)(2,1)S(1)} %shard_map.89), channel_id=1, source_target_pairs={{0,6},{1,15},{2,4},{3,13},{4,10},{5,3},{6,8},{7,1},{8,14},{9,7},{1... | collective-permute-start | bytes 393224 | tf_op jit(solution)/shard_map/ppermute | solution.py:196
  70.2 8.9 %collective-permute-start.18 = (bf16[32,2048]{1,0:T(8,128)(2,1)S(1)}, bf16[32,2048]{1,0:T(8,128)(2,1)S(1)}, u32[]{:S(2)}, u32[]{:S(2)}) collective-permute-start(bf16[32,2048]{1,0:T(8,128)(2,1)S(1)} %shard_map.89), channel_id=1, source_target_pairs={{0,4},{1,13},{2,6},{3,15},{4,8},{5,1},{6,10},{7,3},{8,12},{9,5},{1... | collective-permute-start | bytes 393224 | tf_op jit(solution)/shard_map/ppermute | solution.py:196
  70.2 8.9 %collective-permute-start.16 = (bf16[16,2048]{1,0:T(8,128)(2,1)S(1)}, bf16[16,2048]{1,0:T(8,128)(2,1)S(1)}, u32[]{:S(2)}, u32[]{:S(2)}) collective-permute-start(bf16[16,2048]{1,0:T(8,128)(2,1)S(1)} %get-tuple-element.36.a_ref.refs_0_), channel_id=1, source_target_pairs={{0,2},{1,3},{2,0},{3,1},{4,6},{5,7},{6,4},{7,5},{8,10},{9,11},{10,... | collective-permute-start | bytes 196616 | tf_op jit(solution)/shard_map/ppermute | solution.py:196
  78.5 2.0 %collective-permute-start.24 = (bf16[32,2048]{1,0:T(8,128)(2,1)S(1)}, bf16[32,2048]{1,0:T(8,128)(2,1)S(1)}, u32[]{:S(2)}, u32[]{:S(2)}) collective-permute-start(bf16[32,2048]{1,0:T(8,128)(2,1)S(1)} %collective-permute-done.20.refs_4_), channel_id=1, source_target_pairs={{0,1},{1,0},{2,3},{3,2},{4,5},{5,4},{6,7},{7,6},{8,9},{9,8},{10,11... | collective-permute-start | bytes 393224 | tf_op jit(solution)/shard_map/ppermute | solution.py:196
  78.5 2.0 %collective-permute-start.23 = (bf16[32,2048]{1,0:T(8,128)(2,1)S(1)}, bf16[32,2048]{1,0:T(8,128)(2,1)S(1)}, u32[]{:S(2)}, u32[]{:S(2)}) collective-permute-start(bf16[32,2048]{1,0:T(8,128)(2,1)S(1)} %collective-permute-done.19.refs_3_), channel_id=1, source_target_pairs={{0,1},{1,0},{2,3},{3,2},{4,5},{5,4},{6,7},{7,6},{8,9},{9,8},{10,11... | collective-permute-start | bytes 393224 | tf_op jit(solution)/shard_map/ppermute | solution.py:196
  79.0 1.5 %collective-permute-start.22 = (bf16[32,2048]{1,0:T(8,128)(2,1)S(1)}, bf16[32,2048]{1,0:T(8,128)(2,1)S(1)}, u32[]{:S(2)}, u32[]{:S(2)}) collective-permute-start(bf16[32,2048]{1,0:T(8,128)(2,1)S(1)} %collective-permute-done.18.refs_2_), channel_id=1, source_target_pairs={{0,1},{1,0},{2,3},{3,2},{4,5},{5,4},{6,7},{7,6},{8,9},{9,8},{10,11... | collective-permute-start | bytes 393224 | tf_op jit(solution)/shard_map/ppermute | solution.py:196
  79.1 1.4 %collective-permute-start.21 = (bf16[16,2048]{1,0:T(8,128)(2,1)S(1)}, bf16[16,2048]{1,0:T(8,128)(2,1)S(1)}, u32[]{:S(2)}, u32[]{:S(2)}) collective-permute-start(bf16[16,2048]{1,0:T(8,128)(2,1)S(1)} %collective-permute-done.16.refs_1_), channel_id=1, source_target_pairs={{0,1},{1,0},{2,3},{3,2},{4,5},{5,4},{6,7},{7,6},{8,9},{9,8},{10,11... | collective-permute-start | bytes 196616 | tf_op jit(solution)/shard_map/ppermute | solution.py:196
  80.5 0.8 copy-start.17
  86.8 2.0 %collective-permute-start.25 = (bf16[128,2048]{1,0:T(8,128)(2,1)S(1)}, bf16[128,2048]{1,0:T(8,128)(2,1)S(1)}, u32[]{:S(2)}, u32[]{:S(2)}) collective-permute-start(bf16[128,2048]{1,0:T(8,128)(2,1)S(1)} %get-tuple-element.39), channel_id=1, source_target_pairs={{0,1},{1,0},{2,3},{3,2},{4,5},{5,4},{6,7},{7,6},{8,9},{9,8},{10,11... | collective-permute-start | bytes 1572872 | tf_op jit(solution)/shard_map/ppermute | solution.py:196
  88.9 12.2 %collective-permute-start.27 = (bf16[32,2048]{1,0:T(8,128)(2,1)S(1)}, bf16[32,2048]{1,0:T(8,128)(2,1)S(1)}, u32[]{:S(2)}, u32[]{:S(2)}) collective-permute-start(bf16[32,2048]{1,0:T(8,128)(2,1)S(1)} %get-tuple-element.42), channel_id=1, source_target_pairs={{4,0},{13,1},{6,2},{15,3},{8,4},{1,5},{10,6},{3,7},{12,8},{5,9},{1... | collective-permute-start | bytes 393224 | tf_op jit(solution)/shard_map/ppermute | solution.py:196
  91.6 9.6 %collective-permute-start.28 = (bf16[32,2048]{1,0:T(8,128)(2,1)S(1)}, bf16[32,2048]{1,0:T(8,128)(2,1)S(1)}, u32[]{:S(2)}, u32[]{:S(2)}) collective-permute-start(bf16[32,2048]{1,0:T(8,128)(2,1)S(1)} %get-tuple-element.43), channel_id=1, source_target_pairs={{6,0},{15,1},{4,2},{13,3},{10,4},{3,5},{8,6},{1,7},{14,8},{7,9},{1... | collective-permute-start | bytes 393224 | tf_op jit(solution)/shard_map/ppermute | solution.py:196
  93.8 11.1 %collective-permute-start.29 = (bf16[32,2048]{1,0:T(8,128)(2,1)S(1)}, bf16[32,2048]{1,0:T(8,128)(2,1)S(1)}, u32[]{:S(2)}, u32[]{:S(2)}) collective-permute-start(bf16[32,2048]{1,0:T(8,128)(2,1)S(1)} %get-tuple-element.44), channel_id=1, source_target_pairs={{8,0},{11,1},{10,2},{9,3},{12,4},{15,5},{14,6},{13,7},{0,8},{3,9},... | collective-permute-start | bytes 393224 | tf_op jit(solution)/shard_map/ppermute | solution.py:196
  93.8 7.4 %collective-permute-start.26 = (bf16[16,2048]{1,0:T(8,128)(2,1)S(1)}, bf16[16,2048]{1,0:T(8,128)(2,1)S(1)}, u32[]{:S(2)}, u32[]{:S(2)}) collective-permute-start(bf16[16,2048]{1,0:T(8,128)(2,1)S(1)} %get-tuple-element.41), channel_id=1, source_target_pairs={{0,2},{1,3},{2,0},{3,1},{4,6},{5,7},{6,4},{7,5},{8,10},{9,11},{10,... | collective-permute-start | bytes 196616 | tf_op jit(solution)/shard_map/ppermute | solution.py:196
  105.0 1.3 %collective-permute-start.30 = (bf16[16,2048]{1,0:T(8,128)(2,1)S(1)}, bf16[16,2048]{1,0:T(8,128)(2,1)S(1)}, u32[]{:S(2)}, u32[]{:S(2)}) collective-permute-start(bf16[16,2048]{1,0:T(8,128)(2,1)S(1)} %get-tuple-element.46), channel_id=1, source_target_pairs={{0,1},{1,0},{2,3},{3,2},{4,5},{5,4},{6,7},{7,6},{8,9},{9,8},{10,11... | collective-permute-start | bytes 196616 | tf_op jit(solution)/shard_map/ppermute | solution.py:196

commit v2 on v1

--- a/solution.py
+++ b/solution.py
@@ -10,7 +10,8 @@
 epsilon = 1e-06
 LANES = 128
 VMEM = pl.BlockSpec(memory_space=pltpu.VMEM)
-SMEM = pl.BlockSpec(memory_space=pltpu.SMEM)
+HBM = pl.BlockSpec(memory_space=pltpu.HBM)
+ANY = pl.BlockSpec(memory_space=pl.ANY)
 
 
 def params(mib):
@@ -47,11 +48,24 @@
     return (values * scale * gain_row).astype(jnp.bfloat16)
 
 
-def first_kernel(experts, x_ref, gain_ref, ids_ref, blend_ref, out_ref):
-    rows, features = x_ref.shape
-    ticks, top = ids_ref.shape[0], ids_ref.shape[2]
+def column(row):
+    count = row.shape[1]
+    above = lax.broadcasted_iota(jnp.int32, (count, count), 0)
+    across = lax.broadcasted_iota(jnp.int32, (count, count), 1)
+    return jnp.sum(jnp.where(above == across, row, jnp.zeros_like(row)), axis=1, keepdims=True)
+
+
+def first_kernel(experts, x_hbm, gain_hbm, ids_hbm, blend_hbm, out_ref, state_ref, gain_ref, ids_ref, blend_ref, sems):
+    pairs = ((x_hbm, state_ref), (gain_hbm, gain_ref), (ids_hbm, ids_ref), (blend_hbm, blend_ref))
+    copies = [pltpu.make_async_copy(a, b, sems.at[i]) for i, (a, b) in enumerate(pairs)]
+    for copy in copies:
+        copy.start()
+    for copy in copies:
+        copy.wait()
+    rows, features = state_ref.shape
+    ticks, top = ids_ref.shape[0], ids_ref.shape[1]
     extra = out_ref.shape[1] - features
-    out_ref[:, :features] = rms(x_ref[...].astype(jnp.float32), gain_ref[...])
+    out_ref[:, :features] = rms(state_ref[...].astype(jnp.float32), gain_ref[...])
     lane = lax.broadcasted_iota(jnp.int32, (rows, extra), 1)
     expert = lane % experts
     value = jnp.zeros((rows, extra), jnp.float32)
@@ -60,18 +74,27 @@
         blend = blend_ref[tick]
         mine = lane // (2 * experts) == tick
         for k in range(top):
-            hit = jnp.logical_and(mine, expert == ids[:, k : k + 1])
-            value = value + jnp.where(hit, blend[:, k : k + 1], 0.0)
+            hit = jnp.logical_and(mine, expert == column(ids[k : k + 1]))
+            value = value + jnp.where(hit, column(blend[k : k + 1]), 0.0)
     high = value.astype(jnp.bfloat16).astype(jnp.float32)
     low = value - high
     upper = (lane // experts) % 2 == 0
     out_ref[:, features:] = jnp.where(upper, high, low).astype(jnp.bfloat16)
 
 
-def next_kernel(section_ref, fed_ref, passed_ref, gain_ref, out_ref, state_ref):
-    state = jnp.where(section_ref[0] == 0, fed_ref[...].astype(jnp.float32), passed_ref[...].astype(jnp.float32))
+def next_kernel(fed_ref, passed_ref, gain_ref, out_ref, state_ref):
+    state = jnp.where(lax.axis_index("pipe") == 0, fed_ref[...].astype(jnp.float32), passed_ref[...].astype(jnp.float32))
     state_ref[...] = state.astype(jnp.bfloat16)
     out_ref[...] = rms(state, gain_ref[...])
+
+
+def load_kernel(*refs):
+    count = len(refs) // 2
+    copies = [pltpu.make_async_copy(refs[i], refs[count + i], refs[-1].at[i]) for i in range(count)]
+    for copy in copies:
+        copy.start()
+    for copy in copies:
+        copy.wait()
 
 
 def join_kernel(a_ref, b_ref, out_ref):
@@ -80,7 +103,7 @@
     out_ref[rows:] = b_ref[...]
 
 
-def expert_kernel(tick, experts, pieces, mine_ref, *refs):
+def expert_kernel(tick, experts, pieces, *refs):
     blocks = refs[:pieces]
     refs = refs[pieces:]
     if tick:
@@ -107,7 +130,7 @@
     def _(part):
         span = pl.ds(pl.multiple_of(part * step, step), step)
         lane = lax.broadcasted_iota(jnp.int32, (step, extra), 1)
-        wanted = jnp.logical_and(lane // (2 * experts) == tick, lane % experts == mine_ref[0])
+        wanted = jnp.logical_and(lane // (2 * experts) == tick, lane % experts == lax.axis_index("expert"))
         factor = jnp.sum(jnp.where(wanted, factor_ref[span].astype(jnp.float32), 0.0), axis=1, keepdims=True)
         rows = rows_ref[span]
         for tile in range(hidden // wide):
@@ -154,15 +177,18 @@
     out_ref[len(earlier), 0] = (mine_ref[...] + got_ref[...].astype(jnp.float32)).astype(jnp.bfloat16)
 
 
-def call(kernel, outs, *args, smem=0, scratch=(), mib=32):
+def call(kernel, outs, *args, spec=VMEM, scratch=(), mib=8, cost=None):
     single = not isinstance(outs, (list, tuple))
+    if spec is HBM:
+        args = [pltpu.with_memory_space_constraint(arg, pltpu.HBM) for arg in args]
     return pl.pallas_call(
         kernel,
         out_shape=outs,
-        in_specs=[SMEM] * smem + [VMEM] * (len(args) - smem),
+        in_specs=[spec] * len(args),
         out_specs=VMEM if single else [VMEM] * len(outs),
         scratch_shapes=list(scratch),
         compiler_params=params(mib),
+        cost_estimate=cost and pl.CostEstimate(flops=cost, bytes_accessed=0, transcendentals=0),
     )(*args)
 
 
@@ -183,8 +209,6 @@
     experts = lax.axis_size("expert")
     sections = lax.axis_size("pipe")
     plan = Plan(experts)
-    mine = lax.axis_index("expert").astype(jnp.int32).reshape(1)
-    section = lax.axis_index("pipe").astype(jnp.int32).reshape(1)
     rows, features = resident_batchlets.shape[1:]
     ticks = picked_specialist_ids.shape[0]
     extra = -(-2 * ticks * experts // LANES) * LANES
@@ -200,44 +224,59 @@
     outputs = []
     for tick in range(ticks):
         if tick == 0:
-            normed = call(
+            ids = jnp.swapaxes(picked_specialist_ids[:, 0], 1, 2)
+            blend = jnp.swapaxes(blend_factors[:, 0], 1, 2)
+            normed, state = call(
                 functools.partial(first_kernel, experts),
-                shape(rows, features + extra),
+                [shape(rows, features + extra), shape(rows, features)],
                 state,
                 segment_rms_gain,
-                picked_specialist_ids[:, 0],
-                blend_factors[:, 0],
+                ids,
+                blend,
+                spec=HBM,
+                scratch=[
+                    pltpu.VMEM(segment_rms_gain.shape, jnp.float32),
+                    pltpu.VMEM(ids.shape, jnp.int32),
+                    pltpu.VMEM(blend.shape, jnp.float32),
+                    pltpu.SemaphoreType.DMA((4,)),
+                ],
             )
         else:
             passed = lax.ppermute(outputs[-1], "pipe", [(i, i + 1) for i in range(sections - 1)])
             normed, state = call(
                 next_kernel,
                 [shape(rows, features), shape(rows, features)],
-                section,
                 incoming_batchlets[tick - 1],
                 passed,
                 segment_rms_gain,
-                smem=1,
             )
         width = normed.shape[1]
         beside = move(normed, plan.side)
         partner = move(normed, plan.core)
         chip = call(join_kernel, shape(2 * rows, width), normed, partner)
         far = [move(chip, perm) for perm in plan.far]
+        if tick == 0:
+            weights = call(
+                load_kernel,
+                [shape(*w.shape) for w in weights],
+                *weights,
+                spec=HBM,
+                scratch=[pltpu.SemaphoreType.DMA((3,))],
+                cost=3000000000,
+            )
         direct = [normed, beside] + far
         relayed = [partner] + [move(block, plan.core) for block in direct[1:]]
         blocks = direct + relayed
         outs = [shape(total // 2, features), shape(total // 2, features)]
         if tick == 0:
             outs.append(shape(total, extra))
-        args = [mine] + blocks + ([factors] if tick else []) + list(weights)
+        args = blocks + ([factors] if tick else []) + list(weights)
         got = call(
             functools.partial(expert_kernel, tick, experts, len(blocks)),
             outs,
             *args,
-            smem=1,
             scratch=[pltpu.VMEM((total, features), jnp.bfloat16), pltpu.VMEM((total, hidden), jnp.bfloat16)],
-            mib=48,
+            mib=16,
         )
         keep, send = got[:2]
         if tick == 0:
@@ -249,7 +288,7 @@
             keep,
             swapped,
         )
-        far = [move(block, perm) for block, perm in zip(far, plan.back)]
+        far = [move(block, perm) for block, perm in reversed(list(zip(far, plan.back)))][::-1]
         side = move(side, plan.side)
         part, other = call(
             functools.partial(gather_kernel, len(far)),

time: 108 us -> 89.4 us (0.83)
  local copies, waits for them, and re-layouts: 16 us -> 0.01 us
  Pallas kernels: 12.6 us -> 11.5 us
    unnamed x44 -> x4, local copies, waits for them, and re-layouts: 16 us -> 0.01 us
    pallas_call x12 -> x13, Pallas kernels: 12.6 us -> 11.5 us  [call(): pl.pallas_call(kernel, out_shape=outs, in_specs=[spec] * len(args), out_s...]
  transfers between devices with their start and end apart: 31 -> 31, of which waited for: 17 -> 16; matrix products, arithmetic and copies ran while one was open for 0% -> 0% of each run, Pallas kernels for 0% -> 4%
where the time goes in v2:
time: 89.4 us; the launch traced here: 89.2 us
  waiting for transfers between devices  45 us (50%)
  starting transfers between devices  32.5 us (36%)
  Pallas kernels  11.5 us (13%)
    ppermute x30, waiting for transfers between devices, move(): return lax.ppermute(value, 'expert', perm)  43.2 us
    ppermute x30, starting transfers between devices, move(): return lax.ppermute(value, 'expert', perm)  29.1 us
    pallas_call x13, Pallas kernels, call(): pl.pallas_call(kernel, out_shape=outs, in_specs=[spec] * len(args), out_s...  11.5 us
    ppermute x1, starting transfers between devices, local(): lax.ppermute(outputs[-1], 'pipe', [(i, i + 1) for i in range(sections - 1)])  3.43 us
    ppermute x1, waiting for transfers between devices, local(): lax.ppermute(outputs[-1], 'pipe', [(i, i + 1) for i in range(sections - 1)])  1.88 us
  transfers between devices with their start and end apart: 31, of which 16 were waited for; matrix products, arithmetic and copies ran while one was open for 0% of the time, Pallas kernels for 4%

profile of v2, /device:TPU:0, one launch (start us, length us, event | category | flops | bytes accessed | tf_op | source)
XLA Modules:
  0.0 89.2 jit_solution(16589420865935035695)
XLA Ops:
  0.0 1.1 %shard_map.82 = (bf16[16,2176]{1,0:T(8,128)(2,1)S(1)}, bf16[16,2048]{1,0:T(8,128)(2,1)S(1)}) custom-call(bf16[16,2048]{1,0:T(8,128)(2,1)} %bitcast.12, f32[1,2048]{1,0:T(1,128)} %gain_ref.1, s32[2,8,16]{2,1,0:T(8,128)} %bitcast.13, f32[2,8,16]{2,1,0:T(8,128)} %bitcast.14), custom_call_target="tpu_custom_call" | custom-call | tf_op jit(solution)/shard_map/pallas_call | solution.py:184
  1.1 0.6 collective-permute-start.1
  1.6 0.9 %collective-permute-done.1.b_ref.refs_5_ = bf16[16,2176]{1,0:T(8,128)(2,1)S(1)} collective-permute-done((bf16[16,2176]{1,0:T(8,128)(2,1)S(1)}, bf16[16,2176]{1,0:T(8,128)(2,1)S(1)}, u32[]{:S(2)}, u32[]{:S(2)}) %collective-permute-start.1) | collective-permute-done | bytes 69664 | tf_op jit(solution)/shard_map/ppermute | solution.py:220
  2.6 4.0 %collective-permute-start.4 = (bf16[32,2176]{1,0:T(8,128)(2,1)S(1)}, bf16[32,2176]{1,0:T(8,128)(2,1)S(1)}, u32[]{:S(2)}, u32[]{:S(2)}) collective-permute-start(bf16[32,2176]{1,0:T(8,128)(2,1)S(1)} %shard_map.83), channel_id=1, source_target_pairs={{0,8},{1,11},{2,10},{3,9},{4,12},{5,15},{6,14},{7,13},{8,0},{9,3},... | collective-permute-start | bytes 417800 | tf_op jit(solution)/shard_map/ppermute | solution.py:220
  6.6 2.5 %collective-permute-start.3 = (bf16[32,2176]{1,0:T(8,128)(2,1)S(1)}, bf16[32,2176]{1,0:T(8,128)(2,1)S(1)}, u32[]{:S(2)}, u32[]{:S(2)}) collective-permute-start(bf16[32,2176]{1,0:T(8,128)(2,1)S(1)} %shard_map.83), channel_id=1, source_target_pairs={{0,6},{1,15},{2,4},{3,13},{4,10},{5,3},{6,8},{7,1},{8,14},{9,7},{1... | collective-permute-start | bytes 417800 | tf_op jit(solution)/shard_map/ppermute | solution.py:220
  9.1 0.0 collective-permute-start.2
  9.1 0.6 collective-permute-start
  9.6 5.6 %collective-permute-done.refs_1_ = bf16[16,2176]{1,0:T(8,128)(2,1)S(1)} collective-permute-done((bf16[16,2176]{1,0:T(8,128)(2,1)S(1)}, bf16[16,2176]{1,0:T(8,128)(2,1)S(1)}, u32[]{:S(2)}, u32[]{:S(2)}) %collective-permute-start) | collective-permute-done | bytes 69664 | tf_op jit(solution)/shard_map/ppermute | solution.py:220
  15.3 0.0 collective-permute-start.5
  15.3 0.0 collective-permute-done.4.refs_4_
  15.3 0.5 collective-permute-start.8
  15.8 0.6 collective-permute-done.3.refs_3_
  16.4 2.1 %collective-permute-done.2.refs_2_ = bf16[32,2176]{1,0:T(8,128)(2,1)S(1)} collective-permute-done((bf16[32,2176]{1,0:T(8,128)(2,1)S(1)}, bf16[32,2176]{1,0:T(8,128)(2,1)S(1)}, u32[]{:S(2)}, u32[]{:S(2)}) %collective-permute-start.2) | collective-permute-done | bytes 139296 | tf_op jit(solution)/shard_map/ppermute | solution.py:220
  18.4 3.8 %shard_map.84 = (bf16[2048,768]{1,0:T(8,128)(2,1)S(1)}, bf16[2048,768]{1,0:T(8,128)(2,1)S(1)}, bf16[768,2048]{1,0:T(8,128)(2,1)S(1)}) custom-call(bf16[2048,768]{1,0:T(8,128)(2,1)} %bitcast.15, bf16[2048,768]{1,0:T(8,128)(2,1)} %bitcast.16, bf16[768,2048]{1,0:T(8,128)(2,1)} %bitcast.17), custom_call_target="tpu_custom_call" | custom-call | flops 3000000000 | tf_op jit(solution)/shard_map/pallas_call | solution.py:184
  22.2 0.0 collective-permute-done.5.refs_6_
  22.2 0.0 collective-permute-done.8.refs_9_
  22.3 0.0 collective-permute-done.6.refs_7_
  22.3 0.0 copy-start
  22.3 0.0 copy-start.1
  22.3 2.7 %shard_map.85 = (bf16[128,2048]{1,0:T(8,128)(2,1)S(1)}, bf16[128,2048]{1,0:T(8,128)(2,1)S(1)}, bf16[256,128]{1,0:T(8,128)(2,1)S(1)}) custom-call(bf16[16,2176]{1,0:T(8,128)(2,1)S(1)} %get-tuple-element.32.a_ref.refs_0_, bf16[16,2176]{1,0:T(8,128)(2,1)S(1)} %collective-permute-done.refs_1_, bf16[32,2176]{1,0:T(8,128)(2,1)S(1)} %collective-permute-done.2.refs_2_, ...), custom_call_target="tpu_custom_call" | custom-call | tf_op jit(solution)/shard_map/pallas_call | solution.py:184
  25.0 0.6 collective-permute-start.9
  25.6 1.5 %collective-permute-done.9.got_ref = bf16[128,2048]{1,0:T(8,128)(2,1)S(1)} collective-permute-done((bf16[128,2048]{1,0:T(8,128)(2,1)S(1)}, bf16[128,2048]{1,0:T(8,128)(2,1)S(1)}, u32[]{:S(2)}, u32[]{:S(2)}) %collective-permute-start.9) | collective-permute-done | bytes 524320 | tf_op jit(solution)/shard_map/ppermute | solution.py:220
  27.1 0.1 shard_map.86
  27.3 3.8 %collective-permute-start.11 = (bf16[32,2048]{1,0:T(8,128)(2,1)S(1)}, bf16[32,2048]{1,0:T(8,128)(2,1)S(1)}, u32[]{:S(2)}, u32[]{:S(2)}) collective-permute-start(bf16[32,2048]{1,0:T(8,128)(2,1)S(1)} %get-tuple-element.40), channel_id=1, source_target_pairs={{4,0},{13,1},{6,2},{15,3},{8,4},{1,5},{10,6},{3,7},{12,8},{5,9},{1... | collective-permute-start | bytes 393224 | tf_op jit(solution)/shard_map/ppermute | solution.py:220
  31.1 2.3 %collective-permute-start.12 = (bf16[32,2048]{1,0:T(8,128)(2,1)S(1)}, bf16[32,2048]{1,0:T(8,128)(2,1)S(1)}, u32[]{:S(2)}, u32[]{:S(2)}) collective-permute-start(bf16[32,2048]{1,0:T(8,128)(2,1)S(1)} %get-tuple-element.41), channel_id=1, source_target_pairs={{6,0},{15,1},{4,2},{13,3},{10,4},{3,5},{8,6},{1,7},{14,8},{7,9},{1... | collective-permute-start | bytes 393224 | tf_op jit(solution)/shard_map/ppermute | solution.py:220
  33.4 0.0 collective-permute-start.13
  33.4 1.4 %collective-permute-start.10 = (bf16[16,2048]{1,0:T(8,128)(2,1)S(1)}, bf16[16,2048]{1,0:T(8,128)(2,1)S(1)}, u32[]{:S(2)}, u32[]{:S(2)}) collective-permute-start(bf16[16,2048]{1,0:T(8,128)(2,1)S(1)} %get-tuple-element.39), channel_id=1, source_target_pairs={{0,2},{1,3},{2,0},{3,1},{4,6},{5,7},{6,4},{7,5},{8,10},{9,11},{10,... | collective-permute-start | bytes 196616 | tf_op jit(solution)/shard_map/ppermute | solution.py:220
  34.8 5.4 %collective-permute-done.10.side_ref = bf16[16,2048]{1,0:T(8,128)(2,1)S(1)} collective-permute-done((bf16[16,2048]{1,0:T(8,128)(2,1)S(1)}, bf16[16,2048]{1,0:T(8,128)(2,1)S(1)}, u32[]{:S(2)}, u32[]{:S(2)}) %collective-permute-start.10) | collective-permute-done | bytes 65568 | tf_op jit(solution)/shard_map/ppermute | solution.py:220
  40.2 0.0 collective-permute-done.11.refs_0_
  40.2 0.0 collective-permute-done.12.refs_1_
  40.2 3.4 %collective-permute-done.13.refs_2_ = bf16[32,2048]{1,0:T(8,128)(2,1)S(1)} collective-permute-done((bf16[32,2048]{1,0:T(8,128)(2,1)S(1)}, bf16[32,2048]{1,0:T(8,128)(2,1)S(1)}, u32[]{:S(2)}, u32[]{:S(2)}) %collective-permute-start.13) | collective-permute-done | bytes 131104 | tf_op jit(solution)/shard_map/ppermute | solution.py:220
  43.6 0.1 shard_map.87
  43.7 0.1 collective-permute-start.14
  43.8 1.2 %collective-permute-done.14.got_ref = bf16[16,2048]{1,0:T(8,128)(2,1)S(1)} collective-permute-done((bf16[16,2048]{1,0:T(8,128)(2,1)S(1)}, bf16[16,2048]{1,0:T(8,128)(2,1)S(1)}, u32[]{:S(2)}, u32[]{:S(2)}) %collective-permute-start.14) | collective-permute-done | bytes 65568 | tf_op jit(solution)/shard_map/ppermute | solution.py:220
  45.0 3.4 %collective-permute-start.15 = (bf16[16,2048]{1,0:T(8,128)(2,1)S(1)}, bf16[16,2048]{1,0:T(8,128)(2,1)S(1)}, u32[]{:S(2)}, u32[]{:S(2)}) collective-permute-start(bf16[16,2048]{1,0:T(8,128)(2,1)S(1)} %shard_map.88.refs_0_), channel_id=1, source_target_pairs={{0,16},{1,17},{2,18},{3,19},{4,20},{5,21},{6,22},{7,23},{8,24},{9,... | collective-permute-start | bytes 196616 | tf_op jit(solution)/shard_map/ppermute | solution.py:245
  48.5 1.9 %collective-permute-done.15.passed_ref = bf16[16,2048]{1,0:T(8,128)(2,1)S(1)} collective-permute-done((bf16[16,2048]{1,0:T(8,128)(2,1)S(1)}, bf16[16,2048]{1,0:T(8,128)(2,1)S(1)}, u32[]{:S(2)}, u32[]{:S(2)}) %collective-permute-start.15) | collective-permute-done | bytes 65568 | tf_op jit(solution)/shard_map/ppermute | solution.py:245
  50.3 0.1 shard_map.89
  50.5 0.1 collective-permute-start.17
  50.6 1.2 %collective-permute-done.17.b_ref.refs_5_ = bf16[16,2048]{1,0:T(8,128)(2,1)S(1)} collective-permute-done((bf16[16,2048]{1,0:T(8,128)(2,1)S(1)}, bf16[16,2048]{1,0:T(8,128)(2,1)S(1)}, u32[]{:S(2)}, u32[]{:S(2)}) %collective-permute-start.17) | collective-permute-done | bytes 65568 | tf_op jit(solution)/shard_map/ppermute | solution.py:220
  51.8 0.5 collective-permute-start.20
  52.4 3.8 %collective-permute-start.19 = (bf16[32,2048]{1,0:T(8,128)(2,1)S(1)}, bf16[32,2048]{1,0:T(8,128)(2,1)S(1)}, u32[]{:S(2)}, u32[]{:S(2)}) collective-permute-start(bf16[32,2048]{1,0:T(8,128)(2,1)S(1)} %shard_map.90), channel_id=1, source_target_pairs={{0,6},{1,15},{2,4},{3,13},{4,10},{5,3},{6,8},{7,1},{8,14},{9,7},{1... | collective-permute-start | bytes 393224 | tf_op jit(solution)/shard_map/ppermute | solution.py:220
  56.2 0.0 collective-permute-start.18
  56.2 0.7 collective-permute-start.16
  56.8 7.5 %collective-permute-done.20.refs_4_ = bf16[32,2048]{1,0:T(8,128)(2,1)S(1)} collective-permute-done((bf16[32,2048]{1,0:T(8,128)(2,1)S(1)}, bf16[32,2048]{1,0:T(8,128)(2,1)S(1)}, u32[]{:S(2)}, u32[]{:S(2)}) %collective-permute-start.20) | collective-permute-done | bytes 131104 | tf_op jit(solution)/shard_map/ppermute | solution.py:220
  64.4 0.0 collective-permute-start.24
  64.4 0.0 collective-permute-done.19.refs_3_
  64.4 0.5 collective-permute-start.23
  64.9 0.0 collective-permute-done.18.refs_2_
  64.9 0.1 collective-permute-start.22
  65.0 0.4 collective-permute-start.21
  65.4 0.9 %collective-permute-done.21.refs_6_ = bf16[16,2048]{1,0:T(8,128)(2,1)S(1)} collective-permute-done((bf16[16,2048]{1,0:T(8,128)(2,1)S(1)}, bf16[16,2048]{1,0:T(8,128)(2,1)S(1)}, u32[]{:S(2)}, u32[]{:S(2)}) %collective-permute-start.21) | collective-permute-done | bytes 65568 | tf_op jit(solution)/shard_map/ppermute | solution.py:220
  66.3 2.7 %shard_map.91 = (bf16[128,2048]{1,0:T(8,128)(2,1)S(1)}, bf16[128,2048]{1,0:T(8,128)(2,1)S(1)}) custom-call(bf16[16,2048]{1,0:T(8,128)(2,1)S(1)} %get-tuple-element.46.a_ref.refs_0_, bf16[16,2048]{1,0:T(8,128)(2,1)S(1)} %collective-permute-done.16.refs_1_, bf16[32,2048]{1,0:T(8,128)(2,1)S(1)} %collective-permute-done.18.refs_2_, ...), custom_call_target="tpu_custom_call" | custom-call | tf_op jit(solution)/shard_map/pallas_call | solution.py:184
  69.0 0.4 collective-permute-start.25
  69.4 1.6 %collective-permute-done.25.got_ref = bf16[128,2048]{1,0:T(8,128)(2,1)S(1)} collective-permute-done((bf16[128,2048]{1,0:T(8,128)(2,1)S(1)}, bf16[128,2048]{1,0:T(8,128)(2,1)S(1)}, u32[]{:S(2)}, u32[]{:S(2)}) %collective-permute-start.25) | collective-permute-done | bytes 524320 | tf_op jit(solution)/shard_map/ppermute | solution.py:220
  71.0 0.1 shard_map.92
  71.1 2.8 %collective-permute-start.27 = (bf16[32,2048]{1,0:T(8,128)(2,1)S(1)}, bf16[32,2048]{1,0:T(8,128)(2,1)S(1)}, u32[]{:S(2)}, u32[]{:S(2)}) collective-permute-start(bf16[32,2048]{1,0:T(8,128)(2,1)S(1)} %get-tuple-element.52), channel_id=1, source_target_pairs={{4,0},{13,1},{6,2},{15,3},{8,4},{1,5},{10,6},{3,7},{12,8},{5,9},{1... | collective-permute-start | bytes 393224 | tf_op jit(solution)/shard_map/ppermute | solution.py:220
  73.9 2.0 %collective-permute-start.28 = (bf16[32,2048]{1,0:T(8,128)(2,1)S(1)}, bf16[32,2048]{1,0:T(8,128)(2,1)S(1)}, u32[]{:S(2)}, u32[]{:S(2)}) collective-permute-start(bf16[32,2048]{1,0:T(8,128)(2,1)S(1)} %get-tuple-element.53), channel_id=1, source_target_pairs={{6,0},{15,1},{4,2},{13,3},{10,4},{3,5},{8,6},{1,7},{14,8},{7,9},{1... | collective-permute-start | bytes 393224 | tf_op jit(solution)/shard_map/ppermute | solution.py:220
  75.9 1.4 %collective-permute-start.26 = (bf16[16,2048]{1,0:T(8,128)(2,1)S(1)}, bf16[16,2048]{1,0:T(8,128)(2,1)S(1)}, u32[]{:S(2)}, u32[]{:S(2)}) collective-permute-start(bf16[16,2048]{1,0:T(8,128)(2,1)S(1)} %get-tuple-element.51), channel_id=1, source_target_pairs={{0,2},{1,3},{2,0},{3,1},{4,6},{5,7},{6,4},{7,5},{8,10},{9,11},{10,... | collective-permute-start | bytes 196616 | tf_op jit(solution)/shard_map/ppermute | solution.py:220
  77.3 6.1 %collective-permute-done.26.side_ref = bf16[16,2048]{1,0:T(8,128)(2,1)S(1)} collective-permute-done((bf16[16,2048]{1,0:T(8,128)(2,1)S(1)}, bf16[16,2048]{1,0:T(8,128)(2,1)S(1)}, u32[]{:S(2)}, u32[]{:S(2)}) %collective-permute-start.26) | collective-permute-done | bytes 65568 | tf_op jit(solution)/shard_map/ppermute | solution.py:220
  83.4 3.7 %collective-permute-done.29.refs_2_ = bf16[32,2048]{1,0:T(8,128)(2,1)S(1)} collective-permute-done((bf16[32,2048]{1,0:T(8,128)(2,1)S(1)}, bf16[32,2048]{1,0:T(8,128)(2,1)S(1)}, u32[]{:S(2)}, u32[]{:S(2)}) %collective-permute-start.29) | collective-permute-done | bytes 131104 | tf_op jit(solution)/shard_map/ppermute | solution.py:220
  87.1 0.1 shard_map.93
  87.2 0.1 collective-permute-start.30
  87.3 1.2 %collective-permute-done.30.got_ref = bf16[16,2048]{1,0:T(8,128)(2,1)S(1)} collective-permute-done((bf16[16,2048]{1,0:T(8,128)(2,1)S(1)}, bf16[16,2048]{1,0:T(8,128)(2,1)S(1)}, u32[]{:S(2)}, u32[]{:S(2)}) %collective-permute-start.30) | collective-permute-done | bytes 65568 | tf_op jit(solution)/shard_map/ppermute | solution.py:220
  88.5 0.7 shard_map.94
  (15 shorter events, 0.1 us)
Async XLA Ops:
  1.1 1.5 %collective-permute-start.1 = (bf16[16,2176]{1,0:T(8,128)(2,1)S(1)}, bf16[16,2176]{1,0:T(8,128)(2,1)S(1)}, u32[]{:S(2)}, u32[]{:S(2)}) collective-permute-start(bf16[16,2176]{1,0:T(8,128)(2,1)S(1)} %get-tuple-element.32.a_ref.refs_0_), channel_id=1, source_target_pairs={{0,1},{1,0},{2,3},{3,2},{4,5},{5,4},{6,7},{7,6},{8,9},{9,8},{10,11... | collective-permute-start | bytes 208904 | tf_op jit(solution)/shard_map/ppermute | solution.py:220
  2.6 12.7 %collective-permute-start.4 = (bf16[32,2176]{1,0:T(8,128)(2,1)S(1)}, bf16[32,2176]{1,0:T(8,128)(2,1)S(1)}, u32[]{:S(2)}, u32[]{:S(2)}) collective-permute-start(bf16[32,2176]{1,0:T(8,128)(2,1)S(1)} %shard_map.83), channel_id=1, source_target_pairs={{0,8},{1,11},{2,10},{3,9},{4,12},{5,15},{6,14},{7,13},{8,0},{9,3},... | collective-permute-start | bytes 417800 | tf_op jit(solution)/shard_map/ppermute | solution.py:220
  6.6 9.8 %collective-permute-start.3 = (bf16[32,2176]{1,0:T(8,128)(2,1)S(1)}, bf16[32,2176]{1,0:T(8,128)(2,1)S(1)}, u32[]{:S(2)}, u32[]{:S(2)}) collective-permute-start(bf16[32,2176]{1,0:T(8,128)(2,1)S(1)} %shard_map.83), channel_id=1, source_target_pairs={{0,6},{1,15},{2,4},{3,13},{4,10},{5,3},{6,8},{7,1},{8,14},{9,7},{1... | collective-permute-start | bytes 417800 | tf_op jit(solution)/shard_map/ppermute | solution.py:220
  9.1 9.4 %collective-permute-start.2 = (bf16[32,2176]{1,0:T(8,128)(2,1)S(1)}, bf16[32,2176]{1,0:T(8,128)(2,1)S(1)}, u32[]{:S(2)}, u32[]{:S(2)}) collective-permute-start(bf16[32,2176]{1,0:T(8,128)(2,1)S(1)} %shard_map.83), channel_id=1, source_target_pairs={{0,4},{1,13},{2,6},{3,15},{4,8},{5,1},{6,10},{7,3},{8,12},{9,5},{1... | collective-permute-start | bytes 417800 | tf_op jit(solution)/shard_map/ppermute | solution.py:220
  9.1 6.2 %collective-permute-start = (bf16[16,2176]{1,0:T(8,128)(2,1)S(1)}, bf16[16,2176]{1,0:T(8,128)(2,1)S(1)}, u32[]{:S(2)}, u32[]{:S(2)}) collective-permute-start(bf16[16,2176]{1,0:T(8,128)(2,1)S(1)} %get-tuple-element.32.a_ref.refs_0_), channel_id=1, source_target_pairs={{0,2},{1,3},{2,0},{3,1},{4,6},{5,7},{6,4},{7,5},{8,10},{9,11},{10,... | collective-permute-start | bytes 208904 | tf_op jit(solution)/shard_map/ppermute | solution.py:220
  15.3 7.0 %collective-permute-start.5 = (bf16[16,2176]{1,0:T(8,128)(2,1)S(1)}, bf16[16,2176]{1,0:T(8,128)(2,1)S(1)}, u32[]{:S(2)}, u32[]{:S(2)}) collective-permute-start(bf16[16,2176]{1,0:T(8,128)(2,1)S(1)} %collective-permute-done.refs_1_), channel_id=1, source_target_pairs={{0,1},{1,0},{2,3},{3,2},{4,5},{5,4},{6,7},{7,6},{8,9},{9,8},{10,11... | collective-permute-start | bytes 208904 | tf_op jit(solution)/shard_map/ppermute | solution.py:220
  15.3 7.0 %collective-permute-start.8 = (bf16[32,2176]{1,0:T(8,128)(2,1)S(1)}, bf16[32,2176]{1,0:T(8,128)(2,1)S(1)}, u32[]{:S(2)}, u32[]{:S(2)}) collective-permute-start(bf16[32,2176]{1,0:T(8,128)(2,1)S(1)} %collective-permute-done.4.refs_4_), channel_id=1, source_target_pairs={{0,1},{1,0},{2,3},{3,2},{4,5},{5,4},{6,7},{7,6},{8,9},{9,8},{10,11... | collective-permute-start | bytes 417800 | tf_op jit(solution)/shard_map/ppermute | solution.py:220
  16.4 5.9 %collective-permute-start.7 = (bf16[32,2176]{1,0:T(8,128)(2,1)S(1)}, bf16[32,2176]{1,0:T(8,128)(2,1)S(1)}, u32[]{:S(2)}, u32[]{:S(2)}) collective-permute-start(bf16[32,2176]{1,0:T(8,128)(2,1)S(1)} %collective-permute-done.3.refs_3_), channel_id=1, source_target_pairs={{0,1},{1,0},{2,3},{3,2},{4,5},{5,4},{6,7},{7,6},{8,9},{9,8},{10,11... | collective-permute-start | bytes 417800 | tf_op jit(solution)/shard_map/ppermute | solution.py:220
  18.4 3.8 %collective-permute-start.6 = (bf16[32,2176]{1,0:T(8,128)(2,1)S(1)}, bf16[32,2176]{1,0:T(8,128)(2,1)S(1)}, u32[]{:S(2)}, u32[]{:S(2)}) collective-permute-start(bf16[32,2176]{1,0:T(8,128)(2,1)S(1)} %collective-permute-done.2.refs_2_), channel_id=1, source_target_pairs={{0,1},{1,0},{2,3},{3,2},{4,5},{5,4},{6,7},{7,6},{8,9},{9,8},{10,11... | collective-permute-start | bytes 417800 | tf_op jit(solution)/shard_map/ppermute | solution.py:220
  22.3 28.1 %copy-start = (bf16[1,16,2048]{2,1,0:T(8,128)(2,1)S(1)}, bf16[1,16,2048]{2,1,0:T(8,128)(2,1)}, u32[]{:S(2)}) copy-start(bf16[1,16,2048]{2,1,0:T(8,128)(2,1)} %param.9) | copy-start | bytes 196612
  22.3 28.1 %copy-start.1 = (f32[1,2048]{1,0:T(1,128)S(1)}, f32[1,2048]{1,0:T(1,128)}, u32[]{:S(2)}) copy-start(f32[1,2048]{1,0:T(1,128)} %gain_ref.1) | copy-start | bytes 24580
  25.0 2.1 %collective-permute-start.9 = (bf16[128,2048]{1,0:T(8,128)(2,1)S(1)}, bf16[128,2048]{1,0:T(8,128)(2,1)S(1)}, u32[]{:S(2)}, u32[]{:S(2)}) collective-permute-start(bf16[128,2048]{1,0:T(8,128)(2,1)S(1)} %get-tuple-element.37), channel_id=1, source_target_pairs={{0,1},{1,0},{2,3},{3,2},{4,5},{5,4},{6,7},{7,6},{8,9},{9,8},{10,11... | collective-permute-start | bytes 1572872 | tf_op jit(solution)/shard_map/ppermute | solution.py:220
  27.3 13.0 %collective-permute-start.11 = (bf16[32,2048]{1,0:T(8,128)(2,1)S(1)}, bf16[32,2048]{1,0:T(8,128)(2,1)S(1)}, u32[]{:S(2)}, u32[]{:S(2)}) collective-permute-start(bf16[32,2048]{1,0:T(8,128)(2,1)S(1)} %get-tuple-element.40), channel_id=1, source_target_pairs={{4,0},{13,1},{6,2},{15,3},{8,4},{1,5},{10,6},{3,7},{12,8},{5,9},{1... | collective-permute-start | bytes 393224 | tf_op jit(solution)/shard_map/ppermute | solution.py:220
  31.1 9.1 %collective-permute-start.12 = (bf16[32,2048]{1,0:T(8,128)(2,1)S(1)}, bf16[32,2048]{1,0:T(8,128)(2,1)S(1)}, u32[]{:S(2)}, u32[]{:S(2)}) collective-permute-start(bf16[32,2048]{1,0:T(8,128)(2,1)S(1)} %get-tuple-element.41), channel_id=1, source_target_pairs={{6,0},{15,1},{4,2},{13,3},{10,4},{3,5},{8,6},{1,7},{14,8},{7,9},{1... | collective-permute-start | bytes 393224 | tf_op jit(solution)/shard_map/ppermute | solution.py:220
  33.4 10.2 %collective-permute-start.13 = (bf16[32,2048]{1,0:T(8,128)(2,1)S(1)}, bf16[32,2048]{1,0:T(8,128)(2,1)S(1)}, u32[]{:S(2)}, u32[]{:S(2)}) collective-permute-start(bf16[32,2048]{1,0:T(8,128)(2,1)S(1)} %get-tuple-element.42), channel_id=1, source_target_pairs={{8,0},{11,1},{10,2},{9,3},{12,4},{15,5},{14,6},{13,7},{0,8},{3,9},... | collective-permute-start | bytes 393224 | tf_op jit(solution)/shard_map/ppermute | solution.py:220
  33.4 6.8 %collective-permute-start.10 = (bf16[16,2048]{1,0:T(8,128)(2,1)S(1)}, bf16[16,2048]{1,0:T(8,128)(2,1)S(1)}, u32[]{:S(2)}, u32[]{:S(2)}) collective-permute-start(bf16[16,2048]{1,0:T(8,128)(2,1)S(1)} %get-tuple-element.39), channel_id=1, source_target_pairs={{0,2},{1,3},{2,0},{3,1},{4,6},{5,7},{6,4},{7,5},{8,10},{9,11},{10,... | collective-permute-start | bytes 196616 | tf_op jit(solution)/shard_map/ppermute | solution.py:220
  43.7 1.3 %collective-permute-start.14 = (bf16[16,2048]{1,0:T(8,128)(2,1)S(1)}, bf16[16,2048]{1,0:T(8,128)(2,1)S(1)}, u32[]{:S(2)}, u32[]{:S(2)}) collective-permute-start(bf16[16,2048]{1,0:T(8,128)(2,1)S(1)} %get-tuple-element.44), channel_id=1, source_target_pairs={{0,1},{1,0},{2,3},{3,2},{4,5},{5,4},{6,7},{7,6},{8,9},{9,8},{10,11... | collective-permute-start | bytes 196616 | tf_op jit(solution)/shard_map/ppermute | solution.py:220
  45.0 5.3 %collective-permute-start.15 = (bf16[16,2048]{1,0:T(8,128)(2,1)S(1)}, bf16[16,2048]{1,0:T(8,128)(2,1)S(1)}, u32[]{:S(2)}, u32[]{:S(2)}) collective-permute-start(bf16[16,2048]{1,0:T(8,128)(2,1)S(1)} %shard_map.88.refs_0_), channel_id=1, source_target_pairs={{0,16},{1,17},{2,18},{3,19},{4,20},{5,21},{6,22},{7,23},{8,24},{9,... | collective-permute-start | bytes 196616 | tf_op jit(solution)/shard_map/ppermute | solution.py:245
  50.5 1.3 %collective-permute-start.17 = (bf16[16,2048]{1,0:T(8,128)(2,1)S(1)}, bf16[16,2048]{1,0:T(8,128)(2,1)S(1)}, u32[]{:S(2)}, u32[]{:S(2)}) collective-permute-start(bf16[16,2048]{1,0:T(8,128)(2,1)S(1)} %get-tuple-element.46.a_ref.refs_0_), channel_id=1, source_target_pairs={{0,1},{1,0},{2,3},{3,2},{4,5},{5,4},{6,7},{7,6},{8,9},{9,8},{10,11... | collective-permute-start | bytes 196616 | tf_op jit(solution)/shard_map/ppermute | solution.py:220
  51.8 12.6 %collective-permute-start.20 = (bf16[32,2048]{1,0:T(8,128)(2,1)S(1)}, bf16[32,2048]{1,0:T(8,128)(2,1)S(1)}, u32[]{:S(2)}, u32[]{:S(2)}) collective-permute-start(bf16[32,2048]{1,0:T(8,128)(2,1)S(1)} %shard_map.90), channel_id=1, source_target_pairs={{0,8},{1,11},{2,10},{3,9},{4,12},{5,15},{6,14},{7,13},{8,0},{9,3},... | collective-permute-start | bytes 393224 | tf_op jit(solution)/shard_map/ppermute | solution.py:220
  52.4 12.0 %collective-permute-start.19 = (bf16[32,2048]{1,0:T(8,128)(2,1)S(1)}, bf16[32,2048]{1,0:T(8,128)(2,1)S(1)}, u32[]{:S(2)}, u32[]{:S(2)}) collective-permute-start(bf16[32,2048]{1,0:T(8,128)(2,1)S(1)} %shard_map.90), channel_id=1, source_target_pairs={{0,6},{1,15},{2,4},{3,13},{4,10},{5,3},{6,8},{7,1},{8,14},{9,7},{1... | collective-permute-start | bytes 393224 | tf_op jit(solution)/shard_map/ppermute | solution.py:220
  56.2 8.7 %collective-permute-start.18 = (bf16[32,2048]{1,0:T(8,128)(2,1)S(1)}, bf16[32,2048]{1,0:T(8,128)(2,1)S(1)}, u32[]{:S(2)}, u32[]{:S(2)}) collective-permute-start(bf16[32,2048]{1,0:T(8,128)(2,1)S(1)} %shard_map.90), channel_id=1, source_target_pairs={{0,4},{1,13},{2,6},{3,15},{4,8},{5,1},{6,10},{7,3},{8,12},{9,5},{1... | collective-permute-start | bytes 393224 | tf_op jit(solution)/shard_map/ppermute | solution.py:220
  56.2 8.8 %collective-permute-start.16 = (bf16[16,2048]{1,0:T(8,128)(2,1)S(1)}, bf16[16,2048]{1,0:T(8,128)(2,1)S(1)}, u32[]{:S(2)}, u32[]{:S(2)}) collective-permute-start(bf16[16,2048]{1,0:T(8,128)(2,1)S(1)} %get-tuple-element.46.a_ref.refs_0_), channel_id=1, source_target_pairs={{0,2},{1,3},{2,0},{3,1},{4,6},{5,7},{6,4},{7,5},{8,10},{9,11},{10,... | collective-permute-start | bytes 196616 | tf_op jit(solution)/shard_map/ppermute | solution.py:220
  64.4 2.0 %collective-permute-start.24 = (bf16[32,2048]{1,0:T(8,128)(2,1)S(1)}, bf16[32,2048]{1,0:T(8,128)(2,1)S(1)}, u32[]{:S(2)}, u32[]{:S(2)}) collective-permute-start(bf16[32,2048]{1,0:T(8,128)(2,1)S(1)} %collective-permute-done.20.refs_4_), channel_id=1, source_target_pairs={{0,1},{1,0},{2,3},{3,2},{4,5},{5,4},{6,7},{7,6},{8,9},{9,8},{10,11... | collective-permute-start | bytes 393224 | tf_op jit(solution)/shard_map/ppermute | solution.py:220
  64.4 2.0 %collective-permute-start.23 = (bf16[32,2048]{1,0:T(8,128)(2,1)S(1)}, bf16[32,2048]{1,0:T(8,128)(2,1)S(1)}, u32[]{:S(2)}, u32[]{:S(2)}) collective-permute-start(bf16[32,2048]{1,0:T(8,128)(2,1)S(1)} %collective-permute-done.19.refs_3_), channel_id=1, source_target_pairs={{0,1},{1,0},{2,3},{3,2},{4,5},{5,4},{6,7},{7,6},{8,9},{9,8},{10,11... | collective-permute-start | bytes 393224 | tf_op jit(solution)/shard_map/ppermute | solution.py:220
  64.9 1.5 %collective-permute-start.22 = (bf16[32,2048]{1,0:T(8,128)(2,1)S(1)}, bf16[32,2048]{1,0:T(8,128)(2,1)S(1)}, u32[]{:S(2)}, u32[]{:S(2)}) collective-permute-start(bf16[32,2048]{1,0:T(8,128)(2,1)S(1)} %collective-permute-done.18.refs_2_), channel_id=1, source_target_pairs={{0,1},{1,0},{2,3},{3,2},{4,5},{5,4},{6,7},{7,6},{8,9},{9,8},{10,11... | collective-permute-start | bytes 393224 | tf_op jit(solution)/shard_map/ppermute | solution.py:220
  65.0 1.4 %collective-permute-start.21 = (bf16[16,2048]{1,0:T(8,128)(2,1)S(1)}, bf16[16,2048]{1,0:T(8,128)(2,1)S(1)}, u32[]{:S(2)}, u32[]{:S(2)}) collective-permute-start(bf16[16,2048]{1,0:T(8,128)(2,1)S(1)} %collective-permute-done.16.refs_1_), channel_id=1, source_target_pairs={{0,1},{1,0},{2,3},{3,2},{4,5},{5,4},{6,7},{7,6},{8,9},{9,8},{10,11... | collective-permute-start | bytes 196616 | tf_op jit(solution)/shard_map/ppermute | solution.py:220
  69.0 2.0 %collective-permute-start.25 = (bf16[128,2048]{1,0:T(8,128)(2,1)S(1)}, bf16[128,2048]{1,0:T(8,128)(2,1)S(1)}, u32[]{:S(2)}, u32[]{:S(2)}) collective-permute-start(bf16[128,2048]{1,0:T(8,128)(2,1)S(1)} %get-tuple-element.49), channel_id=1, source_target_pairs={{0,1},{1,0},{2,3},{3,2},{4,5},{5,4},{6,7},{7,6},{8,9},{9,8},{10,11... | collective-permute-start | bytes 1572872 | tf_op jit(solution)/shard_map/ppermute | solution.py:220
  71.1 12.3 %collective-permute-start.27 = (bf16[32,2048]{1,0:T(8,128)(2,1)S(1)}, bf16[32,2048]{1,0:T(8,128)(2,1)S(1)}, u32[]{:S(2)}, u32[]{:S(2)}) collective-permute-start(bf16[32,2048]{1,0:T(8,128)(2,1)S(1)} %get-tuple-element.52), channel_id=1, source_target_pairs={{4,0},{13,1},{6,2},{15,3},{8,4},{1,5},{10,6},{3,7},{12,8},{5,9},{1... | collective-permute-start | bytes 393224 | tf_op jit(solution)/shard_map/ppermute | solution.py:220
  73.9 9.5 %collective-permute-start.28 = (bf16[32,2048]{1,0:T(8,128)(2,1)S(1)}, bf16[32,2048]{1,0:T(8,128)(2,1)S(1)}, u32[]{:S(2)}, u32[]{:S(2)}) collective-permute-start(bf16[32,2048]{1,0:T(8,128)(2,1)S(1)} %get-tuple-element.53), channel_id=1, source_target_pairs={{6,0},{15,1},{4,2},{13,3},{10,4},{3,5},{8,6},{1,7},{14,8},{7,9},{1... | collective-permute-start | bytes 393224 | tf_op jit(solution)/shard_map/ppermute | solution.py:220
  75.9 11.2 %collective-permute-start.29 = (bf16[32,2048]{1,0:T(8,128)(2,1)S(1)}, bf16[32,2048]{1,0:T(8,128)(2,1)S(1)}, u32[]{:S(2)}, u32[]{:S(2)}) collective-permute-start(bf16[32,2048]{1,0:T(8,128)(2,1)S(1)} %get-tuple-element.54), channel_id=1, source_target_pairs={{8,0},{11,1},{10,2},{9,3},{12,4},{15,5},{14,6},{13,7},{0,8},{3,9},... | collective-permute-start | bytes 393224 | tf_op jit(solution)/shard_map/ppermute | solution.py:220
  75.9 7.5 %collective-permute-start.26 = (bf16[16,2048]{1,0:T(8,128)(2,1)S(1)}, bf16[16,2048]{1,0:T(8,128)(2,1)S(1)}, u32[]{:S(2)}, u32[]{:S(2)}) collective-permute-start(bf16[16,2048]{1,0:T(8,128)(2,1)S(1)} %get-tuple-element.51), channel_id=1, source_target_pairs={{0,2},{1,3},{2,0},{3,1},{4,6},{5,7},{6,4},{7,5},{8,10},{9,11},{10,... | collective-permute-start | bytes 196616 | tf_op jit(solution)/shard_map/ppermute | solution.py:220
  87.2 1.3 %collective-permute-start.30 = (bf16[16,2048]{1,0:T(8,128)(2,1)S(1)}, bf16[16,2048]{1,0:T(8,128)(2,1)S(1)}, u32[]{:S(2)}, u32[]{:S(2)}) collective-permute-start(bf16[16,2048]{1,0:T(8,128)(2,1)S(1)} %get-tuple-element.56), channel_id=1, source_target_pairs={{0,1},{1,0},{2,3},{3,2},{4,5},{5,4},{6,7},{7,6},{8,9},{9,8},{10,11... | collective-permute-start | bytes 196616 | tf_op jit(solution)/shard_map/ppermute | solution.py:220
